TPU v7x, 32 devices: a whole 2x2x4 slice. The times are simulated.
32 devices in a mesh: seq: 8 (over y, x, core), batch: 4 (over z).
Axes of the slice: x: 2, y: 2, z: 4, core: 2. Of those that a mesh axis runs over, the one named last changes fastest.
Arguments:
- stream_in: bfloat16 [16, 2048, 768], P('batch', 'seq'), may hold values from -6 to 6
- lengths: int32 [16], P('batch'), may hold values from 64 to 2048, as said below
- token_mask: int32 [16, 2048], P('batch', 'seq'), may hold values from 0 to 1, as said below
- norm1_gain: bfloat16 [768], replicated, may hold values from 0.5 to 1.5
- w_qkv: bfloat16 [768, 2304], replicated, may hold values from -0.21875 to 0.21875
- conv_taps: bfloat16 [3, 2304], replicated, may hold values from -3 to 3
- w_out: bfloat16 [768, 768], replicated, may hold values from -1.75 to 1.75
- norm2_gain: bfloat16 [768], replicated, may hold values from 0.5 to 1.5
- w_up: bfloat16 [768, 3072], replicated, may hold values from -0.21875 to 0.21875
- w_down: bfloat16 [3072, 768], replicated, may hold values from -0.109375 to 0.109375
- grad_output: bfloat16 [16, 2048, 768], P('batch', 'seq'), may hold values from -6 to 6
Outputs:
- stream_out: bfloat16 [16, 2048, 768], P('batch', 'seq')
- grad_input: float32 [16, 2048, 768], P('batch', 'seq')
- grad_norm1: float32 [768], P('batch')
- grad_qkv: float32 [768, 2304], P('batch')
- grad_taps: float32 [3, 2304], replicated
- grad_wout: float32 [768, 768], P('batch')
- grad_norm2: float32 [768], P('batch')
- grad_up: float32 [768, 3072], P('batch')
- grad_down: float32 [3072, 768], P('batch')
- block_rms: float32 [3], replicated
Inputs may be any that keep to these rules, and one draw needn't show every extreme that they name: `lengths`: lengths are heavy tailed over 64 to 2048; some sequence has exactly 2048. `token_mask`: 0 or 1; the first position of every sequence is 1.
All inputs are finite; a program needn't handle non-finite values.
Results may differ from a plain program's by a relative error of at most 0.02.
Values may be sent and summed in bfloat16 or wider, within the bound.
A program may use at most 384 MiB of HBM per device.

v0:
```python
import functools
import math

import jax
import jax.numpy as jnp
from jax import lax
from jax.experimental import pallas as pl
from jax.experimental.pallas import tpu as pltpu
from jax.sharding import PartitionSpec as P

HEADS = 12
HEAD = 64
PAIRS = HEADS // 2
WIDE = 2 * HEAD
TILE = 256
NEG = -1e30
F32 = jnp.float32
BF16 = jnp.bfloat16


def mm(left_op, right_op):
    return jnp.dot(left_op, right_op, preferred_element_type=F32)


def mm_nt(left_op, right_op):
    return lax.dot_general(
        left_op, right_op, (((1,), (1,)), ((), ())), preferred_element_type=F32
    )


def mm_tn(left_op, right_op):
    return lax.dot_general(
        left_op, right_op, (((0,), (0,)), ((), ())), preferred_element_type=F32
    )


def params(limit):
    return pltpu.CompilerParams(vmem_limit_bytes=limit << 20)


def project_kernel(x_ref, gain_ref, w_ref, n_ref, p_ref):
    x = x_ref[0].astype(F32)
    factor = lax.rsqrt(jnp.mean(x * x, axis=-1, keepdims=True) + 1e-06)
    normed = (x * factor * gain_ref[...].astype(F32)).astype(BF16)
    n_ref[0] = normed
    width = x.shape[1]
    for part in range(3):
        cols = mm(normed, w_ref[:, part * width : (part + 1) * width])
        for pair in range(PAIRS):
            p_ref[pair, :, part * WIDE : (part + 1) * WIDE] = cols[
                :, pair * WIDE : (pair + 1) * WIDE
            ].astype(BF16)


def project(x, gain, w_qkv):
    groups, rows, width = x.shape
    return pl.pallas_call(
        project_kernel,
        grid=(groups,),
        in_specs=[
            pl.BlockSpec((1, rows, width), lambda s: (s, 0, 0)),
            pl.BlockSpec((1, width), lambda s: (0, 0)),
            pl.BlockSpec(w_qkv.shape, lambda s: (0, 0)),
        ],
        out_specs=[
            pl.BlockSpec((1, rows, width), lambda s: (s, 0, 0)),
            pl.BlockSpec((PAIRS, rows, 3 * WIDE), lambda s: (s, 0, 0)),
        ],
        out_shape=[
            jax.ShapeDtypeStruct(x.shape, BF16),
            jax.ShapeDtypeStruct((groups * PAIRS, rows, 3 * WIDE), BF16),
        ],
        compiler_params=params(40),
        name="project",
    )(x, gain.reshape(1, width), w_qkv)


def stack_heads(rows):
    lane = lax.broadcasted_iota(jnp.int32, rows.shape, 1)
    zero = jnp.zeros_like(rows)
    first = jnp.where(lane < HEAD, rows, zero)
    second = jnp.where(lane < HEAD, zero, rows)
    return jnp.concatenate([first, second], axis=0)


def unstack_heads(rows):
    half = rows.shape[0] // 2
    lane = lax.broadcasted_iota(jnp.int32, (half, rows.shape[1]), 1)
    return jnp.where(lane < HEAD, rows[:half], rows[half:])


def tile_rows(index):
    return pl.ds(pl.multiple_of(index * TILE, TILE), TILE)


def allowed_keys(key_tile, query_tile, length):
    shape = (TILE, 2 * TILE)
    k_pos = key_tile * TILE + lax.broadcasted_iota(jnp.int32, shape, 0)
    q_pos = query_tile * TILE + (lax.broadcasted_iota(jnp.int32, shape, 1) & (TILE - 1))
    return (k_pos <= q_pos) & (k_pos < length)


def over_key_tiles(query_tile, length, visit):
    full = jnp.minimum(query_tile, length // TILE)
    last = jnp.minimum(query_tile + 1, (length + TILE - 1) // TILE)

    def plain(key_tile, carry):
        visit(key_tile, False)
        return carry

    def edge(key_tile, carry):
        visit(key_tile, True)
        return carry

    lax.fori_loop(0, full, plain, 0)
    lax.fori_loop(full, last, edge, 0)


def convolve(wide_ref, taps_ref, tile):
    begin = 8 + tile * TILE
    total = taps_ref[0:1] * wide_ref[begin : begin + TILE]
    total += taps_ref[1:2] * wide_ref[begin - 1 : begin - 1 + TILE]
    total += taps_ref[2:3] * wide_ref[begin - 2 : begin - 2 + TILE]
    return total


def attend_kernel(info, p_ref, taps_ref, o_ref, lse_ref, wide, q_sc, k_sc, vt_sc, m_sc, acc):
    length = info[0]
    tiles = p_ref.shape[0] // TILE
    taps = taps_ref.at[0]
    wide[0:8] = jnp.zeros((8, wide.shape[1]), F32)
    wide[8:] = p_ref[...].astype(F32)
    for tile in range(tiles):
        rows = slice(tile * TILE, (tile + 1) * TILE)
        mixed = convolve(wide, taps, tile).astype(BF16)
        q_sc[rows] = mixed[:, :WIDE] * (1.0 / math.sqrt(HEAD))
        k_sc[rows] = mixed[:, WIDE : 2 * WIDE]
        vt_sc[tile, :WIDE] = mixed[:, 2 * WIDE :].astype(F32).T.astype(BF16)
        vt_sc[tile, WIDE:] = jnp.ones((vt_sc.shape[1] - WIDE, TILE), BF16)

    def query_tile(index, carry):
        q_stack = stack_heads(q_sc[tile_rows(index)])
        m_sc[...] = jnp.full(m_sc.shape, NEG, F32)
        acc[...] = jnp.zeros(acc.shape, F32)

        def visit(key_tile, masked):
            scores = mm_nt(k_sc[tile_rows(key_tile)], q_stack)
            if masked:
                scores = jnp.where(allowed_keys(key_tile, index, length), scores, NEG)
            old = m_sc[...]
            new = jnp.maximum(old, jnp.max(scores, axis=0, keepdims=True))
            probs = jnp.exp(scores - new)
            acc[...] = acc[...] * jnp.exp(old - new) + mm(vt_sc[key_tile], probs.astype(BF16))
            m_sc[...] = new

        over_key_tiles(index, length, visit)
        total = acc[WIDE : WIDE + 1]
        out = (acc[:WIDE] / total).T
        o_ref[tile_rows(index)] = unstack_heads(out).astype(BF16)
        lse_ref[pl.ds(index, 1)] = m_sc[...] + jnp.log(total)
        return carry

    lax.fori_loop(0, tiles, query_tile, 0)


def attend(info, proj, taps):
    rows = proj.shape[0]
    tiles = rows // TILE
    whole = lambda i, info: (0, 0)
    return pl.pallas_call(
        attend_kernel,
        grid_spec=pltpu.PrefetchScalarGridSpec(
            num_scalar_prefetch=1,
            grid=(1,),
            in_specs=[
                pl.BlockSpec((rows, 3 * WIDE), whole),
                pl.BlockSpec((1, 3, 3 * WIDE), lambda i, info: (info[1], 0, 0)),
            ],
            out_specs=[
                pl.BlockSpec((rows, WIDE), whole),
                pl.BlockSpec((tiles, 2 * TILE), whole),
            ],
            scratch_shapes=[
                pltpu.VMEM((rows + 8, 3 * WIDE), F32),
                pltpu.VMEM((rows, WIDE), BF16),
                pltpu.VMEM((rows, WIDE), BF16),
                pltpu.VMEM((tiles, WIDE + 16, TILE), BF16),
                pltpu.VMEM((1, 2 * TILE), F32),
                pltpu.VMEM((WIDE + 16, 2 * TILE), F32),
            ],
        ),
        out_shape=[
            jax.ShapeDtypeStruct((rows, WIDE), BF16),
            jax.ShapeDtypeStruct((tiles, 2 * TILE), F32),
        ],
        compiler_params=params(40),
        name="attend",
    )(info, proj, taps)


def attend_back_kernel(
    info, p_ref, taps_ref, o_ref, do_ref, lse_ref, dp_ref, gt_ref, wide, q_sc, k_sc, v_sc, kt_sc, dm, dqt
):
    length = info[0]
    tiles = p_ref.shape[0] // TILE
    taps = taps_ref.at[0]
    wide[0:8] = jnp.zeros((8, wide.shape[1]), F32)
    wide[8:] = p_ref[...].astype(F32)
    dm[...] = jnp.zeros(dm.shape, F32)
    for tile in range(tiles):
        rows = slice(tile * TILE, (tile + 1) * TILE)

        @pl.when(tile * TILE < length)
        def _():
            mixed = convolve(wide, taps, tile).astype(BF16)
            q_sc[rows] = mixed[:, :WIDE] * (1.0 / math.sqrt(HEAD))
            k_sc[rows] = mixed[:, WIDE : 2 * WIDE]
            v_sc[rows] = mixed[:, 2 * WIDE :]
            kt_sc[tile] = mixed[:, WIDE : 2 * WIDE].astype(F32).T.astype(BF16)

    lane = lax.broadcasted_iota(jnp.int32, (8, WIDE), 1)
    row = lax.broadcasted_iota(jnp.int32, (8, WIDE), 0)
    picks = jnp.where((lane < HEAD) == (row == 0), 1.0, 0.0).astype(BF16)

    def query_tile(index, carry):
        here = tile_rows(index)
        q_stack = stack_heads(q_sc[here])
        d_rows = do_ref[here]
        d_stack = stack_heads(d_rows)
        product = d_rows.astype(F32) * o_ref[here].astype(F32)
        upper = product.astype(BF16)
        lower = (product - upper.astype(F32)).astype(BF16)
        sums = mm_nt(picks, upper) + mm_nt(picks, lower)
        delta = jnp.concatenate([sums[0:1], sums[1:2]], axis=1)
        lse = lse_ref[pl.ds(index, 1)]
        dqt[...] = jnp.zeros(dqt.shape, F32)

        def visit(key_tile, masked):
            there = tile_rows(key_tile)
            scores = mm_nt(k_sc[there], q_stack)
            probs = jnp.exp(scores - lse)
            if masked:
                probs = jnp.where(allowed_keys(key_tile, index, length), probs, 0.0)
            d_probs = mm_nt(v_sc[there], d_stack)
            d_scores = (probs * (d_probs - delta)).astype(BF16)
            dm[there, 2 * WIDE :] += mm(probs.astype(BF16), d_stack)
            dm[there, WIDE : 2 * WIDE] += mm(d_scores, q_stack)
            dqt[...] += mm(kt_sc[key_tile], d_scores)

        over_key_tiles(index, length, visit)
        dm[here, :WIDE] = unstack_heads(dqt[...].T) * (1.0 / math.sqrt(HEAD))
        return carry

    lax.fori_loop(0, (length + TILE - 1) // TILE, query_tile, 0)
    gt_ref[...] = jnp.zeros(gt_ref.shape, F32)
    for tile in range(tiles):
        begin = tile * TILE
        total = taps[0:1] * dm[begin : begin + TILE]
        total += taps[1:2] * dm[begin + 1 : begin + 1 + TILE]
        total += taps[2:3] * dm[begin + 2 : begin + 2 + TILE]
        dp_ref[begin : begin + TILE] = total.astype(BF16)
        for tap in range(3):
            behind = wide[begin + 8 - tap : begin + 8 - tap + TILE]
            gt_ref[tap : tap + 1] += jnp.sum(
                dm[begin : begin + TILE] * behind, axis=0, keepdims=True
            )


def attend_back(info, proj, taps, attended, d_attended, lse):
    rows = proj.shape[0]
    tiles = rows // TILE
    whole = lambda i, info: (0, 0)
    return pl.pallas_call(
        attend_back_kernel,
        grid_spec=pltpu.PrefetchScalarGridSpec(
            num_scalar_prefetch=1,
            grid=(1,),
            in_specs=[
                pl.BlockSpec((rows, 3 * WIDE), whole),
                pl.BlockSpec((1, 3, 3 * WIDE), lambda i, info: (info[1], 0, 0)),
                pl.BlockSpec((rows, WIDE), whole),
                pl.BlockSpec((rows, WIDE), whole),
                pl.BlockSpec((tiles, 2 * TILE), whole),
            ],
            out_specs=[
                pl.BlockSpec((rows, 3 * WIDE), whole),
                pl.BlockSpec((8, 3 * WIDE), whole),
            ],
            scratch_shapes=[
                pltpu.VMEM((rows + 8, 3 * WIDE), F32),
                pltpu.VMEM((rows, WIDE), BF16),
                pltpu.VMEM((rows, WIDE), BF16),
                pltpu.VMEM((rows, WIDE), BF16),
                pltpu.VMEM((tiles, WIDE, TILE), BF16),
                pltpu.VMEM((rows + 8, 3 * WIDE), F32),
                pltpu.VMEM((WIDE, 2 * TILE), F32),
            ],
        ),
        out_shape=[
            jax.ShapeDtypeStruct((rows, 3 * WIDE), BF16),
            jax.ShapeDtypeStruct((8, 3 * WIDE), F32),
        ],
        compiler_params=params(48),
        name="attend_back",
    )(info, proj, taps, attended, d_attended, lse)


def dense_kernel(
    x_ref, att_ref, cot_ref, weight_ref, gain_ref, wo_ref, wu_ref, wd_ref,
    out_ref, dh_ref, datt_ref, n2_ref, sq_ref, du_ref, da_ref, cz_ref, gain_grad_ref, stats_ref,
    act_sc, att_sc,
):
    rows, width = x_ref.shape[1:]
    hidden_units = wu_ref.shape[1]
    step = width
    for pair in range(PAIRS):
        att_sc[:, pair * WIDE : (pair + 1) * WIDE] = att_ref[pair]
    weight = weight_ref[0]
    gain = gain_ref[...].astype(F32)
    branch = mm(att_sc[...], wo_ref[...])
    hidden = x_ref[0].astype(F32) + branch
    factor = lax.rsqrt(jnp.mean(hidden * hidden, axis=-1, keepdims=True) + 1e-06)
    normed = (hidden * factor * gain).astype(BF16)
    n2_ref[0] = normed
    total = jnp.zeros((rows, width), F32)
    for begin in range(0, hidden_units, step):
        cols = slice(begin, begin + step)
        active = jnp.maximum(mm(normed, wu_ref[:, cols]), 0.0)
        act_sc[:, cols] = active
        squared = (active * active).astype(BF16)
        sq_ref[0, :, cols] = squared
        total += mm(squared, wd_ref[cols])
    full = hidden + total
    out_ref[0] = full.astype(BF16)

    def masked(values):
        per_row = jnp.sum(values * values, axis=-1, keepdims=True)
        return jnp.sum(weight * per_row, axis=0, keepdims=True)

    @pl.when(pl.program_id(0) == 0)
    def _():
        stats_ref[...] = jnp.zeros(stats_ref.shape, F32)
        gain_grad_ref[...] = jnp.zeros(gain_grad_ref.shape, F32)

    parts = [masked(full), masked(branch), masked(total), jnp.sum(weight, axis=0, keepdims=True)]
    for place, part in enumerate(parts):
        stats_ref[place : place + 1] += jnp.broadcast_to(part, (1, WIDE))
    cotangent = (cot_ref[0].astype(F32) * weight).astype(BF16)
    cz_ref[0] = cotangent
    d_normed = jnp.zeros((rows, width), F32)
    for begin in range(0, hidden_units, step):
        cols = slice(begin, begin + step)
        d_squared = mm_nt(cotangent, wd_ref[cols])
        d_up = (2.0 * act_sc[:, cols] * d_squared).astype(BF16)
        du_ref[0, :, cols] = d_up
        d_normed += mm_nt(d_up, wu_ref[:, cols])
    weighted = d_normed * gain
    inner = jnp.mean(weighted * hidden, axis=-1, keepdims=True)
    d_hidden = cotangent.astype(F32) + factor * weighted - hidden * (factor * factor * factor) * inner
    gain_grad_ref[...] += jnp.sum(d_normed * hidden * factor, axis=0, keepdims=True)
    dh_ref[0] = d_hidden
    d_attn = d_hidden.astype(BF16)
    da_ref[0] = d_attn
    d_att = mm_nt(d_attn, wo_ref[...]).astype(BF16)
    for pair in range(PAIRS):
        datt_ref[pair] = d_att[:, pair * WIDE : (pair + 1) * WIDE]


def dense(x, attended, grad_output, weight, gain, w_out, w_up, w_down):
    groups, rows, width = x.shape
    hidden_units = w_up.shape[1]
    per_group = lambda s: (s, 0, 0)
    fixed = lambda s: (0, 0)
    once = pl.Buffered(1)
    row_block = pl.BlockSpec((1, rows, width), per_group)
    wide_block = pl.BlockSpec((1, rows, hidden_units), per_group)
    unit_block = pl.BlockSpec((PAIRS, rows, WIDE), per_group)
    low = jax.ShapeDtypeStruct(x.shape, BF16)
    wide_low = jax.ShapeDtypeStruct((groups, rows, hidden_units), BF16)
    return pl.pallas_call(
        dense_kernel,
        grid=(groups,),
        in_specs=[
            row_block,
            unit_block,
            row_block,
            pl.BlockSpec((1, rows, 1), per_group),
            pl.BlockSpec((1, width), fixed),
            pl.BlockSpec(w_out.shape, fixed, pipeline_mode=once),
            pl.BlockSpec(w_up.shape, fixed, pipeline_mode=once),
            pl.BlockSpec(w_down.shape, fixed, pipeline_mode=once),
        ],
        out_specs=[
            row_block,
            row_block,
            unit_block,
            row_block,
            wide_block,
            wide_block,
            row_block,
            row_block,
            pl.BlockSpec((1, width), fixed),
            pl.BlockSpec((8, WIDE), fixed),
        ],
        out_shape=[
            low,
            jax.ShapeDtypeStruct(x.shape, F32),
            jax.ShapeDtypeStruct((groups * PAIRS, rows, WIDE), BF16),
            low,
            wide_low,
            wide_low,
            low,
            low,
            jax.ShapeDtypeStruct((1, width), F32),
            jax.ShapeDtypeStruct((8, WIDE), F32),
        ],
        scratch_shapes=[pltpu.VMEM((rows, hidden_units), F32), pltpu.VMEM((rows, width), BF16)],
        compiler_params=params(58),
        name="dense",
    )(x, attended, grad_output, weight, gain.reshape(1, width), w_out, w_up, w_down)


PART = 384


def feed_grads_kernel(sq_ref, cz_ref, n2_ref, du_ref, att_ref, da_ref, out_ref, n2_t):
    half, sub = pl.program_id(0), pl.program_id(1)
    groups, rows, width = n2_ref.shape
    tokens = groups * rows

    @pl.when((half == 0) & (sub == 0))
    def _():
        for group in range(groups):
            n2_t[:, group * rows : (group + 1) * rows] = n2_ref[group].astype(F32).T.astype(BF16)

    down = mm_tn(sq_ref[...].reshape(tokens, PART), cz_ref[...].reshape(tokens, width))
    for place in range(4):
        for side in range(2):
            out_ref[place, pl.ds(sub, 1), side * 96 : side * 96 + 96] = down[
                place * 96 : (place + 1) * 96, side * PART : (side + 1) * PART
            ].astype(BF16)[None]
    up = mm(n2_t[...], du_ref[...].reshape(tokens, PART))
    out_ref[pl.ds(sub, 1), :, 192:384] = up.astype(BF16).reshape(1, 4, 192, PART)

    @pl.when(sub == 0)
    def _():
        for pair in range(PAIRS):
            block = mm_tn(
                att_ref[:, pair].reshape(tokens, WIDE), da_ref[...].reshape(tokens, PART)
            ).astype(BF16)
            for low in range(0, WIDE, 16):
                row = pair * WIDE + low
                batch, inner = row // 192, row % 192
                out_ref[inner // 48, batch, 384 + inner % 48 : 400 + inner % 48] = block[low : low + 16]


def feed_grads(squared, cotangent, normed2, d_up, attended, d_attn):
    groups, rows, width = normed2.shape
    whole = lambda h, b: (0, 0, 0)
    return pl.pallas_call(
        feed_grads_kernel,
        grid=(2, 4),
        in_specs=[
            pl.BlockSpec((groups, rows, PART), lambda h, b: (0, 0, 2 * b + h)),
            pl.BlockSpec((groups, rows, width), whole, pipeline_mode=pl.Buffered(1)),
            pl.BlockSpec((groups, rows, width), whole, pipeline_mode=pl.Buffered(1)),
            pl.BlockSpec((groups, rows, PART), lambda h, b: (0, 0, 4 * h + b)),
            pl.BlockSpec(
                (groups, PAIRS, rows, WIDE), lambda h, b: (0, 0, 0, 0), pipeline_mode=pl.Buffered(1)
            ),
            pl.BlockSpec((groups, rows, PART), lambda h, b: (0, 0, h)),
        ],
        out_specs=pl.BlockSpec((4, 4, 432, PART), lambda h, b: (h, 0, 0, 0)),
        out_shape=jax.ShapeDtypeStruct((8, 4, 432, PART), BF16),
        scratch_shapes=[pltpu.VMEM((width, groups * rows), BF16)],
        compiler_params=params(58),
        name="feed_grads",
    )(squared, cotangent, normed2, d_up, attended.reshape(groups, PAIRS, rows, WIDE), d_attn)


def input_grads_kernel(
    dp_ref, n1_ref, x_ref, dh_ref, w_ref, gain_ref, out_ref, gx_ref, gain_grad_ref, n1_t, total, w_sc
):
    pair = pl.program_id(0)
    groups, rows, width = n1_ref.shape
    tokens = groups * rows

    @pl.when(pair == 0)
    def _():
        for group in range(groups):
            n1_t[:, group * rows : (group + 1) * rows] = n1_ref[group].astype(F32).T.astype(BF16)
        total[...] = jnp.zeros(total.shape, F32)

    d_proj = dp_ref[...].reshape(tokens, 3 * WIDE)
    grad = mm(n1_t[...], d_proj).astype(BF16)
    for batch in range(4):
        for chip in range(4):
            begin = batch * 192 + chip * 48
            out_ref[0, 0, chip, batch] = grad[begin : begin + 48]
    for part in range(3):
        cols = pl.ds(pl.multiple_of(part * width + pair * WIDE, WIDE), WIDE)
        w_sc[:, part * WIDE : (part + 1) * WIDE] = w_ref[:, cols]
    total[...] += mm_nt(d_proj, w_sc[...])

    @pl.when(pair == PAIRS - 1)
    def _():
        gain = gain_ref[...].astype(F32)
        gain_sum = jnp.zeros((1, width), F32)
        for group in range(groups):
            x = x_ref[group].astype(F32)
            d_normed = total[group * rows : (group + 1) * rows]
            factor = lax.rsqrt(jnp.mean(x * x, axis=-1, keepdims=True) + 1e-06)
            weighted = d_normed * gain
            inner = jnp.mean(weighted * x, axis=-1, keepdims=True)
            gx_ref[group] = (
                dh_ref[group] + factor * weighted - x * (factor * factor * factor) * inner
            )
            gain_sum += jnp.sum(d_normed * x * factor, axis=0, keepdims=True)
        gain_grad_ref[...] = gain_sum


def input_grads(d_proj, normed1, x, d_hidden, w_qkv, gain):
    groups, rows, width = x.shape
    whole = lambda p: (0, 0, 0)
    once = pl.Buffered(1)
    tokens = pl.BlockSpec((groups, rows, width), whole, pipeline_mode=once)
    return pl.pallas_call(
        input_grads_kernel,
        grid=(PAIRS,),
        in_specs=[
            pl.BlockSpec((groups, 1, rows, 3 * WIDE), lambda p: (0, p, 0, 0)),
            tokens,
            tokens,
            tokens,
            pl.BlockSpec(w_qkv.shape, lambda p: (0, 0), pipeline_mode=once),
            pl.BlockSpec((1, width), lambda p: (0, 0)),
        ],
        out_specs=[
            pl.BlockSpec((1, 1, 4, 4, 48, PART), lambda p: (p % 3, p // 3, 0, 0, 0, 0)),
            tokens,
            pl.BlockSpec((1, width), lambda p: (0, 0)),
        ],
        out_shape=[
            jax.ShapeDtypeStruct((3, 2, 4, 4, 48, PART), BF16),
            jax.ShapeDtypeStruct(x.shape, F32),
            jax.ShapeDtypeStruct((1, width), F32),
        ],
        scratch_shapes=[
            pltpu.VMEM((width, groups * rows), BF16),
            pltpu.VMEM((groups * rows, width), F32),
            pltpu.VMEM((width, 3 * WIDE), BF16),
        ],
        compiler_params=params(58),
        name="input_grads",
    )(d_proj.reshape(groups, PAIRS, rows, 3 * WIDE), normed1, x, d_hidden, w_qkv, gain.reshape(1, width))


MESH = pl.DeviceIdType.MESH


def sum_kernel(
    g_ref, feed_ref, small_ref, qkv_out, feed_out, small_out,
    core_in, here, chip_in, mine, z_in, qkv_all, feed_in, feed_all, row_in, row_sum, col_in,
    core_s, core_r, chip_s, chip_r, z_s, z_r, qkv_s, qkv_r, fz_s, fz_r, fa_s, fa_r,
    row_s, row_r, col_s, col_r,
):
    me = lax.axis_index("seq")
    z = lax.axis_index("batch")
    core, chip = lax.rem(me, 2), me // 2
    barrier = pltpu.get_barrier_semaphore()
    for bit in range(1, 8):
        pl.semaphore_signal(barrier, inc=1, device_id={"seq": me ^ bit}, device_id_type=MESH)
    for bit in range(1, 4):
        pl.semaphore_signal(barrier, inc=1, device_id={"batch": z ^ bit}, device_id_type=MESH)
    pl.semaphore_wait(barrier, 10)

    def send(source, target, sems, axis, peer):
        copy = pltpu.make_async_remote_copy(
            src_ref=source,
            dst_ref=target,
            send_sem=sems[0],
            recv_sem=sems[1],
            device_id={axis: peer},
            device_id_type=MESH,
        )
        copy.start()
        return copy

    def spread(ref, s, r):
        return [
            send(ref.at[me], ref.at[me], (s.at[step], r.at[step]), "seq", me ^ max(2 * step, 1))
            for step in range(4)
        ]

    def relay(ref, first, s, r):
        more = []
        for step in range(1, 4):
            first[step].wait()
            slot = me ^ (2 * step)
            more.append(
                send(ref.at[slot], ref.at[slot], (s.at[3 + step], r.at[3 + step]), "seq", me ^ 1)
            )
        return [first[0]] + more

    chunks = g_ref.shape[0]
    rows = feed_ref.shape[1] // chunks
    to_core = [
        send(g_ref.at[c, 1 - core], core_in.at[c], (core_s.at[c], core_r.at[c]), "seq", me ^ 1)
        for c in range(chunks)
    ]
    feed_z = [
        [
            send(
                feed_ref.at[z ^ bit, c * rows : (c + 1) * rows],
                feed_in.at[c, bit - 1],
                (fz_s.at[c, bit - 1], fz_r.at[c, bit - 1]),
                "batch",
                z ^ bit,
            )
            for bit in range(1, 4)
        ]
        for c in range(chunks)
    ]
    row_in[pl.ds(me, 1)] = small_ref[...][None]
    rows_out = [
        send(small_ref, row_in.at[me], (row_s.at[bit - 1], row_r.at[bit - 1]), "seq", me ^ bit)
        for bit in range(1, 8)
    ]
    to_chip = []
    for c in range(chunks):
        to_core[c].wait()
        for q in range(4):
            both = g_ref[c, core, q].astype(F32) + core_in[c, q].astype(F32)
            here[c, q] = both.astype(BF16)
        to_chip.append(
            [
                send(
                    here.at[c, chip ^ bit],
                    chip_in.at[c, bit - 1],
                    (chip_s.at[c, bit - 1], chip_r.at[c, bit - 1]),
                    "seq",
                    me ^ (2 * bit),
                )
                for bit in range(1, 4)
            ]
        )
    for copy in rows_out:
        copy.wait()
    total = row_in[0]
    for place in range(1, 8):
        total = total + row_in[place]
    row_sum[...] = total
    col_in[pl.ds(z, 1)] = total[None]
    cols_out = [
        send(row_sum, col_in.at[z], (col_s.at[bit - 1], col_r.at[bit - 1]), "batch", z ^ bit)
        for bit in range(1, 4)
    ]
    to_z = []
    for c in range(chunks):
        for copy in to_chip[c]:
            copy.wait()
        both = here[c, chip].astype(F32)
        for bit in range(3):
            both = both + chip_in[c, bit].astype(F32)
        mine[c] = both.astype(BF16)
        to_z.append(
            [
                send(
                    mine.at[c, z ^ bit],
                    z_in.at[c, bit - 1],
                    (z_s.at[c, bit - 1], z_r.at[c, bit - 1]),
                    "batch",
                    z ^ bit,
                )
                for bit in range(1, 4)
            ]
        )
    feed_first = []
    for c in range(chunks):
        for copy in feed_z[c]:
            copy.wait()
        both = feed_ref[z, c * rows : (c + 1) * rows].astype(F32)
        for bit in range(3):
            both = both + feed_in[c, bit].astype(F32)
        feed_all[c, pl.ds(me, 1)] = both.astype(BF16)[None]
        feed_first.append(spread(feed_all.at[c], fa_s.at[c], fa_r.at[c]))
    qkv_first = []
    for c in range(chunks):
        for copy in to_z[c]:
            copy.wait()
        both = mine[c, z].astype(F32)
        for bit in range(3):
            both = both + z_in[c, bit].astype(F32)
        qkv_all[c, pl.ds(me, 1)] = both.astype(BF16)[None]
        qkv_first.append(spread(qkv_all.at[c], qkv_s.at[c], qkv_r.at[c]))
    last = []
    for c in range(chunks):
        last += relay(feed_all.at[c], feed_first[c], fa_s.at[c], fa_r.at[c])
    for c in range(chunks):
        last += relay(qkv_all.at[c], qkv_first[c], qkv_s.at[c], qkv_r.at[c])
    for copy in cols_out:
        copy.wait()
    small_out[...] = ((col_in[0] + col_in[1]) + col_in[2]) + col_in[3]
    for copy in last:
        copy.wait()
    qkv_out[...] = qkv_all[...]
    feed_out[...] = feed_all[...]


def sum_over_devices(pieces, feed, small):
    chunks, rows = pieces.shape[0], pieces.shape[4]
    feed_rows = feed.shape[1] // chunks
    vmem = pl.BlockSpec(memory_space=pltpu.VMEM)
    dma = pltpu.SemaphoreType.DMA
    pairs = []
    for shape in [(), (3,), (3,), (7,), (3,), (7,)]:
        pairs += [dma((chunks,) + shape), dma((chunks,) + shape)]
    return pl.pallas_call(
        sum_kernel,
        in_specs=[vmem, vmem, vmem],
        out_specs=[vmem, vmem, vmem],
        out_shape=[
            jax.ShapeDtypeStruct((chunks, 8, rows, PART), BF16),
            jax.ShapeDtypeStruct((chunks, 8, feed_rows, PART), BF16),
            jax.ShapeDtypeStruct(small.shape, F32),
        ],
        scratch_shapes=[
            pltpu.VMEM((chunks, 4, 4, rows, PART), BF16),
            pltpu.VMEM((chunks, 4, 4, rows, PART), BF16),
            pltpu.VMEM((chunks, 3, 4, rows, PART), BF16),
            pltpu.VMEM((chunks, 4, rows, PART), BF16),
            pltpu.VMEM((chunks, 3, rows, PART), BF16),
            pltpu.VMEM((chunks, 8, rows, PART), BF16),
            pltpu.VMEM((chunks, 3, feed_rows, PART), BF16),
            pltpu.VMEM((chunks, 8, feed_rows, PART), BF16),
            pltpu.VMEM((8,) + small.shape, F32),
            pltpu.VMEM(small.shape, F32),
            pltpu.VMEM((4,) + small.shape, F32),
        ]
        + pairs
        + [dma((7,)), dma((7,)), dma((3,)), dma((3,))],
        compiler_params=pltpu.CompilerParams(
            collective_id=0, has_side_effects=True, vmem_limit_bytes=56 << 20
        ),
        name="sum_over_devices",
    )(pieces, feed, small)


def unpack_kernel(feed_ref, qkv_ref, down_ref, up_ref, out_ref, grad_ref):
    down_ref[:, :PART] = feed_ref[0, 0, :96].astype(F32)
    down_ref[:48, PART:] = feed_ref[0, 0, 96:].astype(F32)
    down_ref[48:, PART:] = feed_ref[1, 0, :48].astype(F32)
    up_ref[:96] = feed_ref[1, 0, 48:].astype(F32)
    up_ref[96:] = feed_ref[2, 0, :96].astype(F32)
    out_ref[...] = feed_ref[2, 0, 96:].astype(F32)
    place = pl.program_id(0)

    def put(core):
        for c in range(3):
            for part in range(3):
                begin = part * PAIRS * WIDE + (core * 3 + c) * WIDE
                grad_ref[:, begin : begin + WIDE] = qkv_ref[
                    c, 0, :, part * WIDE : (part + 1) * WIDE
                ].astype(F32)

    for core in range(2):
        pl.when(place % 2 == core)(functools.partial(put, core))


def unpack(feed, qkv):
    return pl.pallas_call(
        unpack_kernel,
        grid=(8,),
        in_specs=[
            pl.BlockSpec((3, 1, 144, PART), lambda r: (0, r, 0, 0)),
            pl.BlockSpec((3, 1, 48, PART), lambda r: (0, r, 0, 0)),
        ],
        out_specs=[
            pl.BlockSpec((96, 2 * PART), lambda r: (r, 0)),
            pl.BlockSpec((192, PART), lambda r: (0, r)),
            pl.BlockSpec((48, PART), lambda r: (r % 4, r // 4)),
            pl.BlockSpec((48, 3 * PAIRS * WIDE), lambda r: (r // 2, 0)),
        ],
        out_shape=[
            jax.ShapeDtypeStruct((768, 2 * PART), F32),
            jax.ShapeDtypeStruct((192, 8 * PART), F32),
            jax.ShapeDtypeStruct((192, 2 * PART), F32),
            jax.ShapeDtypeStruct((192, 3 * PAIRS * WIDE), F32),
        ],
        compiler_params=params(32),
        name="unpack",
    )(feed, qkv)


def exchange(blocks):
    return lax.all_to_all(blocks, "seq", 0, 0, tiled=True)


def plain_gradients(feed, qkv):
    down = feed[:, :, :192].reshape(8, 4, 2, 96, PART).transpose(1, 0, 3, 2, 4)
    up = feed[:, :, 192:384].transpose(1, 2, 0, 3)
    out = feed[:, :, 384:].reshape(2, 4, 4, 48, PART).transpose(2, 1, 3, 0, 4)
    grad = qkv.reshape(3, 2, 4, 4, 48, 3, WIDE).transpose(3, 2, 4, 5, 1, 0, 6)
    return (
        down.reshape(3072, 768),
        up.reshape(768, 3072),
        out.reshape(768, 768),
        grad.reshape(768, 2304),
    )


def shards(
    stream_in,
    lengths,
    token_mask,
    norm1_gain,
    w_qkv,
    conv_taps,
    w_out,
    norm2_gain,
    w_up,
    w_down,
    grad_output,
):
    groups, block_len, width = stream_in.shape
    count = lax.axis_size("seq")
    batches = lax.axis_size("batch")
    place = lax.axis_index("seq")
    units = groups * PAIRS
    slots = -(-units // count)
    spare = slots * count - units
    offset = place * block_len
    taps = conv_taps.astype(F32).reshape(3, 3, PAIRS, WIDE).transpose(2, 0, 1, 3)
    taps = taps.reshape(PAIRS, 3, 3 * WIDE)

    def fill(blocks):
        return jnp.pad(blocks, ((0, spare), (0, 0), (0, 0))) if spare else blocks

    def to_heads(blocks, slot):
        got = exchange(blocks[slot * count : (slot + 1) * count])
        return got.reshape(count * block_len, blocks.shape[2])

    def to_tokens(per_slot):
        got = [exchange(rows.reshape(count, block_len, rows.shape[1])) for rows in per_slot]
        return jnp.concatenate(got, axis=0)[:units]

    infos = []
    for slot in range(slots):
        unit = slot * count + place
        sequence = jnp.minimum(unit // PAIRS, groups - 1)
        length = jnp.where(unit < units, lengths[sequence], 0)
        infos.append(jnp.stack([length, unit % PAIRS]).astype(jnp.int32))

    normed1, proj = project(stream_in, norm1_gain, w_qkv)
    proj = fill(proj)
    unit_proj, unit_out, unit_lse = [], [], []
    for slot in range(slots):
        rows = to_heads(proj, slot)
        out, lse = attend(infos[slot], rows, taps)
        unit_proj.append(rows)
        unit_out.append(out)
        unit_lse.append(lse)
    attended = to_tokens(unit_out)

    positions = offset + jnp.arange(block_len, dtype=jnp.int32)
    inside = (positions[None, :] < lengths[:, None]).astype(F32)
    stat_weight = (token_mask.astype(F32) * inside)[..., None]
    (
        stream_out,
        d_hidden,
        d_blocks,
        normed2,
        squared,
        d_up,
        d_attn,
        cotangent,
        grad_norm2,
        local_stats,
    ) = dense(stream_in, attended, grad_output, stat_weight, norm2_gain, w_out, w_up, w_down)
    d_blocks = fill(d_blocks)
    feed = feed_grads(squared, cotangent, normed2, d_up, attended, d_attn)
    fitted = count == 8 and batches == 4
    if fitted:
        feed = lax.psum_scatter(feed, "seq", scatter_dimension=0, tiled=False)

    back, unit_taps = [], jnp.zeros((PAIRS, 3, 3 * WIDE), F32)
    for slot in range(slots):
        d_rows = to_heads(d_blocks, slot)
        d_proj_rows, part = attend_back(
            infos[slot], unit_proj[slot], taps, unit_out[slot], d_rows, unit_lse[slot]
        )
        back.append(d_proj_rows)
        chosen = jnp.arange(PAIRS)[:, None, None] == infos[slot][1]
        unit_taps = unit_taps + jnp.where(chosen, part[None, :3], 0.0)
    grad_taps = unit_taps.reshape(PAIRS, 3, 3, WIDE).transpose(1, 2, 0, 3).reshape(9, width)
    d_proj = to_tokens(back)
    pieces, grad_input, grad_norm1 = input_grads(
        d_proj, normed1, stream_in, d_hidden, w_qkv, norm1_gain
    )
    stats_row = jnp.pad(local_stats[:4, 0], (0, width - 4)).reshape(1, width)
    small = jnp.concatenate(
        [grad_taps, grad_norm1, grad_norm2, stats_row, jnp.zeros((4, width), F32)], axis=0
    )
    if fitted:
        qkv, feed, small = sum_over_devices(pieces, feed, small)
        total_down, total_up, total_wout, total_qkv = unpack(feed, qkv)
    else:

        def reduce(gradient):
            share = lax.psum_scatter(
                gradient, ("batch", "seq"), scatter_dimension=0, tiled=True
            )
            return lax.all_gather(share, "seq", axis=0, tiled=True).astype(F32)

        total_down, total_up, total_wout, total_qkv = map(reduce, plain_gradients(feed, pieces))
        small = lax.psum(small, ("seq", "batch"))
    share = width // batches
    begin = lax.axis_index("batch") * share
    block_rms = jnp.sqrt(small[11, :3] / (width * small[11, 3]))
    return (
        stream_out,
        grad_input,
        lax.dynamic_slice_in_dim(small[9], begin, share),
        total_qkv,
        small[:9].reshape(3, 3 * width),
        total_wout,
        lax.dynamic_slice_in_dim(small[10], begin, share),
        total_up,
        total_down,
        block_rms,
    )


def solution(mesh):
    tokens = P("batch", "seq", None)
    return jax.shard_map(
        shards,
        mesh=mesh,
        in_specs=(
            tokens,
            P("batch"),
            P("batch", "seq"),
            P(),
            P(),
            P(),
            P(),
            P(),
            P(),
            P(),
            tokens,
        ),
        out_specs=(
            tokens,
            tokens,
            P("batch"),
            P("batch", None),
            P(),
            P("batch", None),
            P("batch"),
            P("batch", None),
            P("batch", None),
            P(),
        ),
        check_vma=False,
    )
```

profile of v0, /device:TPU:0, one launch (start us, length us, event | category | flops | bytes accessed | tf_op | source)
XLA Modules:
  0.0 461.3 jit_solution(5661952880579635035)
XLA Ops:
  7.2 0.7 reshape.128.gain_ref
  7.9 2.0 copy-done
  9.9 1.4 copy-done.1
  11.3 4.7 %project.1 = (bf16[4,256,768]{2,1,0:T(8,128)(2,1)S(1)}, bf16[24,256,384]{2,1,0:T(8,128)(2,1)S(1)}) custom-call(bf16[4,256,768]{2,1,0:T(8,128)(2,1)S(1)} %copy-done.1, bf16[1,768]{1,0:T(2,128)(2,1)S(1)} %reshape.128.gain_ref, bf16[768,2304]{1,0:T(8,128)(2,1)S(1)} %copy-done), custom_call_target="tpu_custom_call" | custom-call | tf_op jit(solution)/shard_map/project/pallas_call | solution.py:57
  16.0 1.8 fusion
  17.8 25.9 %all_to_all.60 = bf16[8,256,384]{2,1,0:T(8,128)(2,1)S(1)} all-to-all(bf16[8,256,384]{2,1,0:T(8,128)(2,1)S(1)} %get-tuple-element.80), channel_id=1, replica_groups=mesh['seq'=8,'batch'=4] {'seq'}, dimensions={0} | all-to-all | bytes 3145728 | tf_op jit(solution)/shard_map/all_to_all | solution.py:796
  43.7 23.4 %all_to_all.61 = bf16[8,256,384]{2,1,0:T(8,128)(2,1)S(1)} all-to-all(bf16[8,256,384]{2,1,0:T(8,128)(2,1)S(1)} %get-tuple-element.79), channel_id=1, replica_groups=mesh['seq'=8,'batch'=4] {'seq'}, dimensions={0} | all-to-all | bytes 3145728 | tf_op jit(solution)/shard_map/all_to_all | solution.py:796
  67.1 4.4 all-to-all-start.4
  71.7 0.6 fusion.3
  73.0 0.1 pad_add_fusion.info
  73.0 20.8 %attend.3 = (bf16[2048,128]{1,0:T(8,128)(2,1)S(1)}, f32[8,512]{1,0:T(8,128)S(1)}) custom-call(s32[2]{0:T(128)S(1)} %pad_add_fusion.info, bf16[2048,384]{1,0:T(8,128)(2,1)S(1)} %bitcast.53, f32[6,3,384]{2,1,0:T(4,128)S(1)} %reshape.150.taps_ref), custom_call_target="tpu_custom_call" | custom-call | tf_op jit(solution)/shard_map/attend/pallas_call | solution.py:170
  93.8 0.8 copy-done.3
  94.6 4.2 all-to-all-start.1
  99.4 0.1 pad_add_fusion.1.info
  99.5 10.6 %attend.4 = (bf16[2048,128]{1,0:T(8,128)(2,1)S(1)}, f32[8,512]{1,0:T(8,128)S(1)}) custom-call(s32[2]{0:T(128)S(1)} %pad_add_fusion.1.info, bf16[2048,384]{1,0:T(8,128)(2,1)S(1)} %bitcast.55, f32[6,3,384]{2,1,0:T(4,128)S(1)} %reshape.150.taps_ref), custom_call_target="tpu_custom_call" | custom-call | tf_op jit(solution)/shard_map/attend/pallas_call | solution.py:170
  110.2 0.8 copy-done.5
  111.0 7.0 %all-to-all-start.3 = ((bf16[8,256,128]{2,1,0:T(8,128)(2,1)}), bf16[8,256,128]{2,1,0:T(8,128)(2,1)}, u32[]{:S(2)}, u32[]{:S(2)}) async-start(bf16[8,256,128]{2,1,0:T(8,128)(2,1)} %bitcast.58), calls=%async_computation.3 | async-start | bytes 1048576 | tf_op jit(solution)/shard_map/all_to_all | solution.py:796
  118.7 15.0 %attend.5 = (bf16[2048,128]{1,0:T(8,128)(2,1)S(1)}, f32[8,512]{1,0:T(8,128)S(1)}) custom-call(s32[2]{0:T(128)S(1)} %pad_add_fusion.2.info, bf16[2048,384]{1,0:T(8,128)(2,1)} %bitcast.14.p_ref, f32[6,3,384]{2,1,0:T(4,128)S(1)} %reshape.150.taps_ref), custom_call_target="tpu_custom_call" | custom-call | tf_op jit(solution)/shard_map/attend/pallas_call | solution.py:170
  133.7 0.8 copy-done.7
  134.5 4.1 all-to-all-start.5
  138.6 0.2 reduce-scatter.2.cloned.1.call-start
  138.9 1.0 copy.23.weight_ref
  140.0 0.6 reshape.138.gain_ref
  140.5 1.9 constant_dynamic-update-slice_fusion.2
  142.4 1.9 constant_dynamic-update-slice_fusion.1
  144.3 4.1 all-to-all-done.5
  148.4 1.9 constant_dynamic-update-slice_fusion.att_ref
  150.2 35.9 %dense.1 = (bf16[4,256,768]{2,1,0:T(8,128)(2,1)}, f32[4,256,768]{2,1,0:T(8,128)}, bf16[24,256,128]{2,1,0:T(8,128)(2,1)}, bf16[4,256,768]{2,1,0:T(8,128)(2,1)}, b...) custom-call(bf16[4,256,768]{2,1,0:T(8,128)(2,1)} %x_ref.5, ...), custom_call_target="tpu_custom_call" | custom-call | tf_op jit(solution)/shard_map/dense/pallas_call | solution.py:380
  186.1 21.8 %feed_grads.1 = bf16[8,4,432,384]{3,2,1,0:T(8,128)(2,1)} custom-call(bf16[4,256,3072]{2,1,0:T(8,128)(2,1)} %get-tuple-element.60.sq_ref, bf16[4,256,768]{2,1,0:T(8,128)(2,1)} %get-tuple-element.61.cz_ref, bf16[4,256,768]{2,1,0:T(8,128)(2,1)} %get-tuple-element.62.n2_ref, bf16[4,256,3072]{2,1,0:T(8,128)(2,1)} %get-tuple-element.63.du_ref, ...), custom_call_target="tpu_custom_call" | custom-call | tf_op jit(solution)/shard_map/feed_grads/pallas_call | solution.py:460
  207.9 2.3 fusion.1
  210.2 12.8 %all_to_all.62 = bf16[8,256,128]{2,1,0:T(8,128)(2,1)} all-to-all(bf16[8,256,128]{2,1,0:T(8,128)(2,1)S(1)} %get-tuple-element.82), channel_id=1, replica_groups=mesh['seq'=8,'batch'=4] {'seq'}, dimensions={0} | all-to-all | bytes 1048576 | tf_op jit(solution)/shard_map/all_to_all | solution.py:796
  223.1 12.8 %all_to_all.63 = bf16[8,256,128]{2,1,0:T(8,128)(2,1)} all-to-all(bf16[8,256,128]{2,1,0:T(8,128)(2,1)S(1)} %get-tuple-element.83), channel_id=1, replica_groups=mesh['seq'=8,'batch'=4] {'seq'}, dimensions={0} | all-to-all | bytes 1048576 | tf_op jit(solution)/shard_map/all_to_all | solution.py:796
  235.9 4.2 all-to-all-start.6
  240.1 1.0 copy-done.8
  241.1 1.0 copy-done.10
  242.1 10.2 %attend_back.5 = (bf16[2048,384]{1,0:T(8,128)(2,1)S(1)}, f32[8,384]{1,0:T(8,128)S(1)}) custom-call(s32[2]{0:T(128)S(1)} %pad_add_fusion.2.info, bf16[2048,384]{1,0:T(8,128)(2,1)} %bitcast.14.p_ref, f32[6,3,384]{2,1,0:T(4,128)S(1)} %reshape.150.taps_ref, bf16[2048,128]{1,0:T(8,128)(2,1)S(1)} %copy-done.8, bf16[2048,128]{1,0:T(8,128)(2,1)S(1)} %bitcast.61, ...), custom_call_target="tpu_custom_call" | custom-call | tf_op jit(solution)/shard_map/attend_back/pallas_call | solution.py:273
  252.4 1.1 copy-done.12
  253.5 2.2 all-to-all-done.6
  255.8 4.3 all-to-all-start.11
  260.1 1.0 copy-done.6
  261.1 1.0 copy-done.9
  262.2 6.6 %attend_back.4 = (bf16[2048,384]{1,0:T(8,128)(2,1)S(1)}, f32[8,384]{1,0:T(8,128)S(1)}) custom-call(s32[2]{0:T(128)S(1)} %pad_add_fusion.1.info, bf16[2048,384]{1,0:T(8,128)(2,1)S(1)} %bitcast.56, f32[6,3,384]{2,1,0:T(4,128)S(1)} %reshape.150.taps_ref, bf16[2048,128]{1,0:T(8,128)(2,1)S(1)} %copy-done.6, bf16[2048,128]{1,0:T(8,128)(2,1)S(1)} %bitcast.60, ...), custom_call_target="tpu_custom_call" | custom-call | tf_op jit(solution)/shard_map/attend_back/pallas_call | solution.py:273
  268.8 1.1 copy-done.11
  269.9 22.5 %all-to-all-done.11 = bf16[8,256,384]{2,1,0:T(8,128)(2,1)} async-done(((bf16[8,256,384]{2,1,0:T(8,128)(2,1)}), bf16[8,256,384]{2,1,0:T(8,128)(2,1)}, u32[]{:S(2)}, u32[]{:S(2)}) %all-to-all-start.11) | async-done | bytes 1572896 | tf_op jit(solution)/shard_map/all_to_all | solution.py:796
  292.4 4.3 all-to-all-start.9
  296.7 1.0 copy-done.4
  297.8 28.1 %attend_back.3 = (bf16[2048,384]{1,0:T(8,128)(2,1)}, f32[8,384]{1,0:T(8,128)S(1)}) custom-call(s32[2]{0:T(128)S(1)} %pad_add_fusion.info, bf16[2048,384]{1,0:T(8,128)(2,1)S(1)} %bitcast.54, f32[6,3,384]{2,1,0:T(4,128)S(1)} %reshape.150.taps_ref, bf16[2048,128]{1,0:T(8,128)(2,1)S(1)} %copy-done.4, bf16[2048,128]{1,0:T(8,128)(2,1)} %bitcast.17.do_ref, ...), custom_call_target="tpu_custom_call" | custom-call | tf_op jit(solution)/shard_map/attend_back/pallas_call | solution.py:273
  325.9 3.8 all-to-all-done.9
  329.7 3.7 all-to-all-start.7
  333.6 0.1 slice_reduce_fusion
  334.0 20.4 %all-to-all-done.7 = bf16[8,256,384]{2,1,0:T(8,128)(2,1)S(1)} async-done(((bf16[8,256,384]{2,1,0:T(8,128)(2,1)}), bf16[8,256,384]{2,1,0:T(8,128)(2,1)S(1)}, u32[]{:S(2)}, u32[]{:S(2)}) %all-to-all-start.7) | async-done | bytes 1572896 | tf_op jit(solution)/shard_map/all_to_all | solution.py:796
  354.4 3.9 pad_maximum_fusion
  358.2 19.7 %input_grads.1 = (bf16[3,2,4,4,48,384]{5,4,3,2,1,0:T(8,128)(2,1)}, f32[4,256,768]{2,1,0:T(8,128)}, f32[1,768]{1,0:T(1,128)}) custom-call(bf16[4,6,256,384]{3,2,1,0:T(8,128)(2,1)} %bitcast.64, bf16[4,256,768]{2,1,0:T(8,128)(2,1)} %copy-done.13, bf16[4,256,768]{2,1,0:T(8,128)(2,1)} %x_ref.5, f32[4,256,768]{2,1,0:T(8,128)} %get-tuple-element.57.dh_ref, ...), custom_call_target="tpu_custom_call" | custom-call | tf_op jit(solution)/shard_map/input_grads/pallas_call | solution.py:527
  378.0 2.0 concatenate.11.small_ref
  380.0 59.8 %sum_over_devices.1 = (bf16[3,8,48,384]{3,2,1,0:T(8,128)(2,1)}, bf16[3,8,144,384]{3,2,1,0:T(8,128)(2,1)}, f32[16,768]{1,0:T(8,128)}) custom-call(bf16[3,2,4,4,48,384]{5,4,3,2,1,0:T(8,128)(2,1)} %get-tuple-element.59.g_ref, bf16[4,432,384]{2,1,0:T(8,128)(2,1)} %bitcast.65, f32[16,768]{1,0:T(8,128)} %concatenate.11.small_ref), custom_call_target="tpu_custom_call" | custom-call | tf_op jit(solution)/shard_map/sum_over_devices/pallas_call | solution.py:718
  439.8 0.8 fusion.2
  440.6 1.3 slice.59
  441.9 1.4 reshape.148
  443.3 0.6 constant_dynamic-slice_fusion.1
  444.0 0.6 constant_dynamic-slice_fusion
  445.2 1.2 sqrt_bitcast_fusion
  446.5 1.7 copy-done.2
  448.2 1.2 copy-done.14
  449.4 4.6 %unpack.1 = (f32[768,768]{1,0:T(8,128)}, f32[192,3072]{1,0:T(8,128)}, f32[192,768]{1,0:T(8,128)}, f32[192,2304]{1,0:T(8,128)}) custom-call(bf16[3,8,144,384]{3,2,1,0:T(8,128)(2,1)S(1)} %copy-done.2, bf16[3,8,48,384]{3,2,1,0:T(8,128)(2,1)S(1)} %copy-done.14), custom_call_target="tpu_custom_call" | custom-call | tf_op jit(solution)/shard_map/unpack/pallas_call | solution.py:771
  (65 shorter events, 0.6 us)
Async XLA Ops:
  7.9 2.0 copy-start
  9.9 1.4 copy-start.1
  11.3 4.7 %copy-start.15 = (bf16[1,768]{1,0:T(2,128)(2,1)}, bf16[1,768]{1,0:T(2,128)(2,1)S(1)}, u32[]{:S(2)}) copy-start(bf16[1,768]{1,0:T(2,128)(2,1)S(1)} %reshape.128.gain_ref) | copy-start | bytes 4612
  16.0 1.8 copy-start.13
  67.1 4.5 copy-start.16
  67.1 4.6 copy-start.17
  67.1 27.5 %all-to-all-start.4 = ((bf16[8,256,384]{2,1,0:T(8,128)(2,1)}), bf16[8,256,384]{2,1,0:T(8,128)(2,1)}, u32[]{:S(2)}, u32[]{:S(2)}) async-start(bf16[8,256,384]{2,1,0:T(8,128)(2,1)} %get-tuple-element.78), calls=%async_computation.4 | async-start | bytes 3145728 | tf_op jit(solution)/shard_map/all_to_all | solution.py:796
  93.8 0.8 copy-start.3
  94.6 16.4 %all-to-all-start.1 = ((bf16[8,256,128]{2,1,0:T(8,128)(2,1)}), bf16[8,256,128]{2,1,0:T(8,128)(2,1)}, u32[]{:S(2)}, u32[]{:S(2)}) async-start(bf16[8,256,128]{2,1,0:T(8,128)(2,1)} %bitcast.57), calls=%async_computation.1 | async-start | bytes 1048576 | tf_op jit(solution)/shard_map/all_to_all | solution.py:796
  110.2 0.8 copy-start.5
  111.0 23.5 %all-to-all-start.3 = ((bf16[8,256,128]{2,1,0:T(8,128)(2,1)}), bf16[8,256,128]{2,1,0:T(8,128)(2,1)}, u32[]{:S(2)}, u32[]{:S(2)}) async-start(bf16[8,256,128]{2,1,0:T(8,128)(2,1)} %bitcast.58), calls=%async_computation.3 | async-start | bytes 1048576 | tf_op jit(solution)/shard_map/all_to_all | solution.py:796
  117.9 20.9 %copy-start.18 = (s32[4,256]{1,0:T(4,128)S(1)}, s32[4,256]{1,0:T(4,128)}, u32[]{:S(2)}) copy-start(s32[4,256]{1,0:T(4,128)} %param.13) | copy-start | bytes 12292
  118.7 21.3 %copy-start.20 = (bf16[768]{0:T(1024)(128)(2,1)S(1)}, bf16[768]{0:T(1024)(128)(2,1)}, u32[]{:S(2)}) copy-start(bf16[768]{0:T(1024)(128)(2,1)} %param.18) | copy-start | bytes 4612
  133.7 0.8 copy-start.7
  134.5 13.9 %all-to-all-start.5 = ((bf16[8,256,128]{2,1,0:T(8,128)(2,1)}), bf16[8,256,128]{2,1,0:T(8,128)(2,1)}, u32[]{:S(2)}, u32[]{:S(2)}) async-start(bf16[8,256,128]{2,1,0:T(8,128)(2,1)} %bitcast.59), calls=%async_computation.5 | async-start | bytes 1048576 | tf_op jit(solution)/shard_map/all_to_all | solution.py:796
  138.6 241.3 %reduce-scatter.2.cloned.1.call-start = ((), (), s32[]{:S(2)}) async-start(), calls=%async_computation.13 | async-start | bytes 11943936 | tf_op jit(solution)/shard_map/reduce_scatter | solution.py:884
  235.9 19.9 %all-to-all-start.6 = ((bf16[8,256,128]{2,1,0:T(8,128)(2,1)}), bf16[8,256,128]{2,1,0:T(8,128)(2,1)}, u32[]{:S(2)}, u32[]{:S(2)}) async-start(bf16[8,256,128]{2,1,0:T(8,128)(2,1)} %get-tuple-element.81), calls=%async_computation.6 | async-start | bytes 1048576 | tf_op jit(solution)/shard_map/all_to_all | solution.py:796
  240.1 1.0 copy-start.8
  241.1 1.0 copy-start.10
  252.4 1.1 copy-start.12
  255.8 36.7 %all-to-all-start.11 = ((bf16[8,256,384]{2,1,0:T(8,128)(2,1)}), bf16[8,256,384]{2,1,0:T(8,128)(2,1)}, u32[]{:S(2)}, u32[]{:S(2)}) async-start(bf16[8,256,384]{2,1,0:T(8,128)(2,1)} %bitcast.63), calls=%async_computation.11 | async-start | bytes 3145728 | tf_op jit(solution)/shard_map/all_to_all | solution.py:796
  260.1 1.0 copy-start.6
  261.1 1.0 copy-start.9
  268.8 1.1 copy-start.11
  292.4 37.3 %all-to-all-start.9 = ((bf16[8,256,384]{2,1,0:T(8,128)(2,1)}), bf16[8,256,384]{2,1,0:T(8,128)(2,1)}, u32[]{:S(2)}, u32[]{:S(2)}) async-start(bf16[8,256,384]{2,1,0:T(8,128)(2,1)} %bitcast.62), calls=%async_computation.9 | async-start | bytes 3145728 | tf_op jit(solution)/shard_map/all_to_all | solution.py:796
  296.7 1.0 copy-start.4
  329.7 3.9 copy-start.21
  329.7 24.7 %all-to-all-start.7 = ((bf16[8,256,384]{2,1,0:T(8,128)(2,1)}), bf16[8,256,384]{2,1,0:T(8,128)(2,1)S(1)}, u32[]{:S(2)}, u32[]{:S(2)}) async-start(bf16[8,256,384]{2,1,0:T(8,128)(2,1)} %bitcast.18), calls=%async_computation.7 | async-start | bytes 3145728 | tf_op jit(solution)/shard_map/all_to_all | solution.py:796
  358.2 19.7 %copy-start.19 = (f32[1,768]{1,0:T(1,128)S(1)}, f32[1,768]{1,0:T(1,128)}, u32[]{:S(2)}) copy-start(f32[1,768]{1,0:T(1,128)} %get-tuple-element.69) | copy-start | bytes 9220
  446.4 1.7 copy-start.2
  448.2 1.2 copy-start.14
Sparse Core Ops, SparseCore 0:
  208.1 117.9 reduce-scatter.1
where the time goes:
time: 465 us; the launch traced here: 461 us
  Pallas kernels  238 us (51%)
  blocking collectives  75 us (16%)
  waiting for transfers between devices  53 us (11%)
  starting transfers between devices  36.4 us (8%)
  local copies, waits for them, and re-layouts  36 us (8%)
  between operations  17.6 us (4%)
  other arithmetic  5.4 us (1%)
    all_to_all x4, blocking collectives, exchange(): return lax.all_to_all(blocks, 'seq', 0, 0, tiled=True)  75 us
    pallas_call x1, Pallas kernels, sum_over_devices(): pl.pallas_call(sum_kernel, in_specs=[vmem, vmem, vmem], out_specs=[vmem,...  59.8 us
    all_to_all x8, waiting for transfers between devices, exchange(): return lax.all_to_all(blocks, 'seq', 0, 0, tiled=True)  53 us
    pallas_call x3, Pallas kernels, attend(): pl.pallas_call(attend_kernel, grid_spec=pltpu.PrefetchScalarGridSpec(num_...  46.4 us
    pallas_call x3, Pallas kernels, attend_back(): pl.pallas_call(attend_back_kernel, grid_spec=pltpu.PrefetchScalarGridSpec...  45 us
    all_to_all x8, starting transfers between devices, exchange(): return lax.all_to_all(blocks, 'seq', 0, 0, tiled=True)  36.2 us
    pallas_call x1, Pallas kernels, dense(): pl.pallas_call(dense_kernel, grid=(groups,), in_specs=[row_block, unit_bl...  35.9 us
    pallas_call x1, Pallas kernels, feed_grads(): pl.pallas_call(feed_grads_kernel, grid=(2, 4), in_specs=[pl.BlockSpec((gr...  21.8 us
  transfers between devices with their start and end apart: 9, of which 5 were waited for; matrix products, arithmetic and copies ran while one was open for 3% of the time, Pallas kernels for 24%

commit v1 on v0

--- a/solution.py
+++ b/solution.py
@@ -36,6 +36,114 @@
 
 def params(limit):
     return pltpu.CompilerParams(vmem_limit_bytes=limit << 20)
+
+
+MESH = pl.DeviceIdType.MESH
+GROUP = 8
+DMA = pltpu.SemaphoreType.DMA
+
+
+def remote(source, target, sems, axis, peer):
+    return pltpu.make_async_remote_copy(
+        src_ref=source,
+        dst_ref=target,
+        send_sem=sems[0],
+        recv_sem=sems[1],
+        device_id={axis: peer},
+        device_id_type=MESH,
+    )
+
+
+def meet_group():
+    me = lax.axis_index("seq")
+    barrier = pltpu.get_barrier_semaphore()
+    for bit in range(1, GROUP):
+        pl.semaphore_signal(barrier, inc=1, device_id={"seq": me ^ bit}, device_id_type=MESH)
+    pl.semaphore_wait(barrier, GROUP - 1)
+
+
+def unit_copy(blocks, inbox, sems, unit):
+    me = lax.axis_index("seq")
+    owner, slot = lax.rem(unit, GROUP), unit // GROUP
+    return owner, remote(
+        blocks.at[unit],
+        inbox.at[slot, me],
+        (sems[0].at[unit], sems[1].at[slot, me ^ owner]),
+        "seq",
+        owner,
+    )
+
+
+def send_unit(blocks, inbox, sems, unit):
+    me = lax.axis_index("seq")
+    owner, copy = unit_copy(blocks, inbox, sems, unit)
+
+    @pl.when(owner != me)
+    def _():
+        copy.start()
+
+    @pl.when(owner == me)
+    def _():
+        slot = unit // GROUP
+        pltpu.make_async_copy(blocks.at[unit], inbox.at[slot, me], sems[1].at[slot, 0]).start()
+
+
+def wait_units(blocks, inbox, sems):
+    me = lax.axis_index("seq")
+    units = blocks.shape[0]
+    for slot in range(units // GROUP):
+        unit = slot * GROUP + me
+        pltpu.make_async_copy(blocks.at[unit], inbox.at[slot, me], sems[1].at[slot, 0]).wait()
+        for bit in range(1, GROUP):
+            remote(
+                blocks.at[unit],
+                inbox.at[slot, me ^ bit],
+                (sems[0].at[unit], sems[1].at[slot, bit]),
+                "seq",
+                me ^ bit,
+            ).wait_recv()
+    for unit in range(units):
+        owner, copy = unit_copy(blocks, inbox, sems, unit)
+        pl.when(owner != me)(copy.wait_send)
+
+
+def block_copies(units, inbox, sems, slot):
+    me = lax.axis_index("seq")
+    return [
+        remote(
+            units.at[slot, me ^ bit],
+            inbox.at[slot * GROUP + me],
+            (sems[0].at[slot, bit], sems[1].at[slot, bit]),
+            "seq",
+            me ^ bit,
+        )
+        for bit in range(1, GROUP)
+    ]
+
+
+def own_block(units, inbox, sems, slot):
+    me = lax.axis_index("seq")
+    return pltpu.make_async_copy(
+        units.at[slot, me], inbox.at[slot * GROUP + me], sems[1].at[slot, 0]
+    )
+
+
+def send_blocks(units, inbox, sems, slot):
+    own_block(units, inbox, sems, slot).start()
+    for copy in block_copies(units, inbox, sems, slot):
+        copy.start()
+
+
+def wait_blocks(units, inbox, sems, slot):
+    own_block(units, inbox, sems, slot).wait()
+    for copy in block_copies(units, inbox, sems, slot):
+        copy.wait()
+
+
+def group_params(number, limit):
+    return pltpu.CompilerParams(
+        collective_id=number, has_side_effects=True, vmem_limit_bytes=limit << 20
+    )
 
 
 def project_kernel(x_ref, gain_ref, w_ref, n_ref, p_ref):
@@ -52,6 +160,45 @@
             ].astype(BF16)
 
 
+def project_send_kernel(x_ref, gain_ref, w_ref, n_ref, inbox, blocks, send_sems, recv_sems):
+    group = pl.program_id(0)
+    sems = (send_sems, recv_sems)
+    pl.when(group == 0)(meet_group)
+    project_kernel(x_ref, gain_ref, w_ref, n_ref, blocks.at[pl.ds(group * PAIRS, PAIRS)])
+    for pair in range(PAIRS):
+        send_unit(blocks, inbox, sems, group * PAIRS + pair)
+    pl.when(group == pl.num_programs(0) - 1)(lambda: wait_units(blocks, inbox, sems))
+
+
+def project_send(x, gain, w_qkv):
+    groups, rows, width = x.shape
+    slots = groups * PAIRS // GROUP
+    return pl.pallas_call(
+        project_send_kernel,
+        grid=(groups,),
+        in_specs=[
+            pl.BlockSpec((1, rows, width), lambda s: (s, 0, 0)),
+            pl.BlockSpec((1, width), lambda s: (0, 0)),
+            pl.BlockSpec(w_qkv.shape, lambda s: (0, 0), pipeline_mode=pl.Buffered(1)),
+        ],
+        out_specs=[
+            pl.BlockSpec((1, rows, width), lambda s: (s, 0, 0)),
+            pl.BlockSpec(memory_space=pl.ANY),
+        ],
+        out_shape=[
+            jax.ShapeDtypeStruct(x.shape, BF16),
+            jax.ShapeDtypeStruct((slots, GROUP, rows, 3 * WIDE), BF16),
+        ],
+        scratch_shapes=[
+            pltpu.VMEM((groups * PAIRS, rows, 3 * WIDE), BF16),
+            DMA((groups * PAIRS,)),
+            DMA((slots, GROUP)),
+        ],
+        compiler_params=group_params(1, 40),
+        name="project_send",
+    )(x, gain.reshape(1, width), w_qkv)
+
+
 def project(x, gain, w_qkv):
     groups, rows, width = x.shape
     return pl.pallas_call(
@@ -125,7 +272,8 @@
 
 
 def attend_kernel(info, p_ref, taps_ref, o_ref, lse_ref, wide, q_sc, k_sc, vt_sc, m_sc, acc):
-    length = info[0]
+    p_ref, o_ref, lse_ref = p_ref.at[0], o_ref.at[0], lse_ref.at[0]
+    length = info[pl.program_id(0), 0]
     tiles = p_ref.shape[0] // TILE
     taps = taps_ref.at[0]
     wide[0:8] = jnp.zeros((8, wide.shape[1]), F32)
@@ -164,21 +312,21 @@
 
 
 def attend(info, proj, taps):
-    rows = proj.shape[0]
+    slots, rows = proj.shape[:2]
     tiles = rows // TILE
-    whole = lambda i, info: (0, 0)
+    own = lambda i, info: (i, 0, 0)
     return pl.pallas_call(
         attend_kernel,
         grid_spec=pltpu.PrefetchScalarGridSpec(
             num_scalar_prefetch=1,
-            grid=(1,),
+            grid=(slots,),
             in_specs=[
-                pl.BlockSpec((rows, 3 * WIDE), whole),
-                pl.BlockSpec((1, 3, 3 * WIDE), lambda i, info: (info[1], 0, 0)),
+                pl.BlockSpec((1, rows, 3 * WIDE), own),
+                pl.BlockSpec((1, 3, 3 * WIDE), lambda i, info: (info[i, 1], 0, 0)),
             ],
             out_specs=[
-                pl.BlockSpec((rows, WIDE), whole),
-                pl.BlockSpec((tiles, 2 * TILE), whole),
+                pl.BlockSpec((1, rows, WIDE), own),
+                pl.BlockSpec((1, tiles, 2 * TILE), own),
             ],
             scratch_shapes=[
                 pltpu.VMEM((rows + 8, 3 * WIDE), F32),
@@ -190,8 +338,8 @@
             ],
         ),
         out_shape=[
-            jax.ShapeDtypeStruct((rows, WIDE), BF16),
-            jax.ShapeDtypeStruct((tiles, 2 * TILE), F32),
+            jax.ShapeDtypeStruct((slots, rows, WIDE), BF16),
+            jax.ShapeDtypeStruct((slots, tiles, 2 * TILE), F32),
         ],
         compiler_params=params(40),
         name="attend",
@@ -201,7 +349,9 @@
 def attend_back_kernel(
     info, p_ref, taps_ref, o_ref, do_ref, lse_ref, dp_ref, gt_ref, wide, q_sc, k_sc, v_sc, kt_sc, dm, dqt
 ):
-    length = info[0]
+    p_ref, o_ref, do_ref, lse_ref = p_ref.at[0], o_ref.at[0], do_ref.at[0], lse_ref.at[0]
+    dp_ref, gt_ref = dp_ref.at[0], gt_ref.at[0]
+    length = info[pl.program_id(0), 0]
     tiles = p_ref.shape[0] // TILE
     taps = taps_ref.at[0]
     wide[0:8] = jnp.zeros((8, wide.shape[1]), F32)
@@ -267,24 +417,24 @@
 
 
 def attend_back(info, proj, taps, attended, d_attended, lse):
-    rows = proj.shape[0]
+    slots, rows = proj.shape[:2]
     tiles = rows // TILE
-    whole = lambda i, info: (0, 0)
+    own = lambda i, info: (i, 0, 0)
     return pl.pallas_call(
         attend_back_kernel,
         grid_spec=pltpu.PrefetchScalarGridSpec(
             num_scalar_prefetch=1,
-            grid=(1,),
+            grid=(slots,),
             in_specs=[
-                pl.BlockSpec((rows, 3 * WIDE), whole),
-                pl.BlockSpec((1, 3, 3 * WIDE), lambda i, info: (info[1], 0, 0)),
-                pl.BlockSpec((rows, WIDE), whole),
-                pl.BlockSpec((rows, WIDE), whole),
-                pl.BlockSpec((tiles, 2 * TILE), whole),
+                pl.BlockSpec((1, rows, 3 * WIDE), own),
+                pl.BlockSpec((1, 3, 3 * WIDE), lambda i, info: (info[i, 1], 0, 0)),
+                pl.BlockSpec((1, rows, WIDE), own),
+                pl.BlockSpec((1, rows, WIDE), own),
+                pl.BlockSpec((1, tiles, 2 * TILE), own),
             ],
             out_specs=[
-                pl.BlockSpec((rows, 3 * WIDE), whole),
-                pl.BlockSpec((8, 3 * WIDE), whole),
+                pl.BlockSpec((1, rows, 3 * WIDE), own),
+                pl.BlockSpec((1, 8, 3 * WIDE), own),
             ],
             scratch_shapes=[
                 pltpu.VMEM((rows + 8, 3 * WIDE), F32),
@@ -297,8 +447,8 @@
             ],
         ),
         out_shape=[
-            jax.ShapeDtypeStruct((rows, 3 * WIDE), BF16),
-            jax.ShapeDtypeStruct((8, 3 * WIDE), F32),
+            jax.ShapeDtypeStruct((slots, rows, 3 * WIDE), BF16),
+            jax.ShapeDtypeStruct((slots, 8, 3 * WIDE), F32),
         ],
         compiler_params=params(48),
         name="attend_back",
@@ -366,6 +516,103 @@
         datt_ref[pair] = d_att[:, pair * WIDE : (pair + 1) * WIDE]
 
 
+def dense_send_kernel(
+    x_ref, units_ref, cot_ref, weight_ref, gain_ref, wo_ref, wu_ref, wd_ref,
+    out_ref, dh_ref, inbox, att_ref, n2_ref, sq_ref, du_ref, da_ref, cz_ref, gain_grad_ref, stats_ref,
+    act_sc, att_sc, att_in, d_blocks, in_s, in_r, out_s, out_r,
+):
+    group = pl.program_id(0)
+    in_sems, out_sems = (in_s, in_r), (out_s, out_r)
+    slots = units_ref.shape[0]
+
+    @pl.when(group == 0)
+    def _():
+        meet_group()
+        for slot in range(slots):
+            send_blocks(units_ref, att_in, in_sems, slot)
+
+    for slot in range(slots):
+        first = slot * GROUP // PAIRS
+        pl.when(group == first)(lambda slot=slot: wait_blocks(units_ref, att_in, in_sems, slot))
+    here = pl.ds(group * PAIRS, PAIRS)
+    att_ref[...] = att_in[here]
+    dense_kernel(
+        x_ref, att_in.at[here], cot_ref, weight_ref, gain_ref, wo_ref, wu_ref, wd_ref,
+        out_ref, dh_ref, d_blocks.at[here], n2_ref, sq_ref, du_ref, da_ref, cz_ref, gain_grad_ref,
+        stats_ref, act_sc, att_sc,
+    )
+    for pair in range(PAIRS):
+        send_unit(d_blocks, inbox, out_sems, group * PAIRS + pair)
+    pl.when(group == pl.num_programs(0) - 1)(lambda: wait_units(d_blocks, inbox, out_sems))
+
+
+def dense_send(x, units, grad_output, weight, gain, w_out, w_up, w_down):
+    groups, rows, width = x.shape
+    hidden_units = w_up.shape[1]
+    slots = groups * PAIRS // GROUP
+    per_group = lambda s: (s, 0, 0)
+    fixed = lambda s: (0, 0)
+    once = pl.Buffered(1)
+    anywhere = pl.BlockSpec(memory_space=pl.ANY)
+    row_block = pl.BlockSpec((1, rows, width), per_group)
+    wide_block = pl.BlockSpec((1, rows, hidden_units), per_group)
+    low = jax.ShapeDtypeStruct(x.shape, BF16)
+    wide_low = jax.ShapeDtypeStruct((groups, rows, hidden_units), BF16)
+    unit_rows = (groups * PAIRS, rows, WIDE)
+    return pl.pallas_call(
+        dense_send_kernel,
+        grid=(groups,),
+        in_specs=[
+            row_block,
+            anywhere,
+            row_block,
+            pl.BlockSpec((1, rows, 1), per_group),
+            pl.BlockSpec((1, width), fixed),
+            pl.BlockSpec(w_out.shape, fixed, pipeline_mode=once),
+            pl.BlockSpec(w_up.shape, fixed, pipeline_mode=once),
+            pl.BlockSpec(w_down.shape, fixed, pipeline_mode=once),
+        ],
+        out_specs=[
+            row_block,
+            row_block,
+            anywhere,
+            pl.BlockSpec((PAIRS, rows, WIDE), per_group),
+            row_block,
+            wide_block,
+            wide_block,
+            row_block,
+            row_block,
+            pl.BlockSpec((1, width), fixed),
+            pl.BlockSpec((8, WIDE), fixed),
+        ],
+        out_shape=[
+            low,
+            jax.ShapeDtypeStruct(x.shape, F32),
+            jax.ShapeDtypeStruct((slots, GROUP, rows, WIDE), BF16),
+            jax.ShapeDtypeStruct(unit_rows, BF16),
+            low,
+            wide_low,
+            wide_low,
+            low,
+            low,
+            jax.ShapeDtypeStruct((1, width), F32),
+            jax.ShapeDtypeStruct((8, WIDE), F32),
+        ],
+        scratch_shapes=[
+            pltpu.VMEM((rows, hidden_units), F32),
+            pltpu.VMEM((rows, width), BF16),
+            pltpu.VMEM(unit_rows, BF16),
+            pltpu.VMEM(unit_rows, BF16),
+            DMA((slots, GROUP)),
+            DMA((slots, GROUP)),
+            DMA((groups * PAIRS,)),
+            DMA((slots, GROUP)),
+        ],
+        compiler_params=group_params(2, 58),
+        name="dense_send",
+    )(x, units, grad_output, weight, gain.reshape(1, width), w_out, w_up, w_down)
+
+
 def dense(x, attended, grad_output, weight, gain, w_out, w_up, w_down):
     groups, rows, width = x.shape
     hidden_units = w_up.shape[1]
@@ -553,9 +800,6 @@
         compiler_params=params(58),
         name="input_grads",
     )(d_proj.reshape(groups, PAIRS, rows, 3 * WIDE), normed1, x, d_hidden, w_qkv, gain.reshape(1, width))
-
-
-MESH = pl.DeviceIdType.MESH
 
 
 def sum_kernel(
@@ -833,65 +1077,52 @@
     taps = conv_taps.astype(F32).reshape(3, 3, PAIRS, WIDE).transpose(2, 0, 1, 3)
     taps = taps.reshape(PAIRS, 3, 3 * WIDE)
 
-    def fill(blocks):
-        return jnp.pad(blocks, ((0, spare), (0, 0), (0, 0))) if spare else blocks
-
-    def to_heads(blocks, slot):
-        got = exchange(blocks[slot * count : (slot + 1) * count])
-        return got.reshape(count * block_len, blocks.shape[2])
-
-    def to_tokens(per_slot):
-        got = [exchange(rows.reshape(count, block_len, rows.shape[1])) for rows in per_slot]
-        return jnp.concatenate(got, axis=0)[:units]
-
-    infos = []
-    for slot in range(slots):
-        unit = slot * count + place
-        sequence = jnp.minimum(unit // PAIRS, groups - 1)
-        length = jnp.where(unit < units, lengths[sequence], 0)
-        infos.append(jnp.stack([length, unit % PAIRS]).astype(jnp.int32))
-
-    normed1, proj = project(stream_in, norm1_gain, w_qkv)
-    proj = fill(proj)
-    unit_proj, unit_out, unit_lse = [], [], []
-    for slot in range(slots):
-        rows = to_heads(proj, slot)
-        out, lse = attend(infos[slot], rows, taps)
-        unit_proj.append(rows)
-        unit_out.append(out)
-        unit_lse.append(lse)
-    attended = to_tokens(unit_out)
+    fitted = count == GROUP and batches == 4 and units % GROUP == 0
+
+    def to_heads(blocks):
+        blocks = jnp.pad(blocks, ((0, spare), (0, 0), (0, 0)))
+        blocks = blocks.reshape((slots, count) + blocks.shape[1:])
+        return jnp.stack([exchange(blocks[slot]) for slot in range(slots)])
+
+    def to_tokens(rows):
+        rows = rows.reshape(slots, count, block_len, rows.shape[2])
+        return jnp.concatenate([exchange(rows[slot]) for slot in range(slots)])[:units]
+
+    unit = jnp.arange(slots) * count + place
+    sequence = jnp.minimum(unit // PAIRS, groups - 1)
+    info = jnp.stack([jnp.where(unit < units, lengths[sequence], 0), unit % PAIRS], axis=1)
+    info = info.astype(jnp.int32)
+
+    if fitted:
+        normed1, proj = project_send(stream_in, norm1_gain, w_qkv)
+    else:
+        normed1, proj = project(stream_in, norm1_gain, w_qkv)
+        proj = to_heads(proj)
+    proj = proj.reshape(slots, count * block_len, 3 * WIDE)
+    unit_out, unit_lse = attend(info, proj, taps)
 
     positions = offset + jnp.arange(block_len, dtype=jnp.int32)
     inside = (positions[None, :] < lengths[:, None]).astype(F32)
     stat_weight = (token_mask.astype(F32) * inside)[..., None]
-    (
-        stream_out,
-        d_hidden,
-        d_blocks,
-        normed2,
-        squared,
-        d_up,
-        d_attn,
-        cotangent,
-        grad_norm2,
-        local_stats,
-    ) = dense(stream_in, attended, grad_output, stat_weight, norm2_gain, w_out, w_up, w_down)
-    d_blocks = fill(d_blocks)
+    rest = (grad_output, stat_weight, norm2_gain, w_out, w_up, w_down)
+    if fitted:
+        blocks = unit_out.reshape(slots, count, block_len, WIDE)
+        stream_out, d_hidden, d_units, attended, *saved = dense_send(stream_in, blocks, *rest)
+    else:
+        attended = to_tokens(unit_out)
+        stream_out, d_hidden, d_units, *saved = dense(stream_in, attended, *rest)
+        d_units = to_heads(d_units)
+    normed2, squared, d_up, d_attn, cotangent, grad_norm2, local_stats = saved
+    d_units = d_units.reshape(slots, count * block_len, WIDE)
     feed = feed_grads(squared, cotangent, normed2, d_up, attended, d_attn)
-    fitted = count == 8 and batches == 4
     if fitted:
         feed = lax.psum_scatter(feed, "seq", scatter_dimension=0, tiled=False)
 
-    back, unit_taps = [], jnp.zeros((PAIRS, 3, 3 * WIDE), F32)
+    back, parts = attend_back(info, proj, taps, unit_out, d_units, unit_lse)
+    unit_taps = jnp.zeros((PAIRS, 3, 3 * WIDE), F32)
     for slot in range(slots):
-        d_rows = to_heads(d_blocks, slot)
-        d_proj_rows, part = attend_back(
-            infos[slot], unit_proj[slot], taps, unit_out[slot], d_rows, unit_lse[slot]
-        )
-        back.append(d_proj_rows)
-        chosen = jnp.arange(PAIRS)[:, None, None] == infos[slot][1]
-        unit_taps = unit_taps + jnp.where(chosen, part[None, :3], 0.0)
+        chosen = jnp.arange(PAIRS)[:, None, None] == info[slot, 1]
+        unit_taps = unit_taps + jnp.where(chosen, parts[slot, None, :3], 0.0)
     grad_taps = unit_taps.reshape(PAIRS, 3, 3, WIDE).transpose(1, 2, 0, 3).reshape(9, width)
     d_proj = to_tokens(back)
     pieces, grad_input, grad_norm1 = input_grads(

time: 465 us -> 436 us (0.938)
  Pallas kernels: 238 us -> 290 us
  waiting for transfers between devices: 53 us -> 17.7 us
  starting transfers between devices: 36.4 us -> 4.7 us
  local copies, waits for them, and re-layouts: 36 us -> 28.8 us
  blocking collectives: 75 us -> 70 us
    pallas_call x2, Pallas kernels: 40.6 us -> 115 us  [the longest x1 57.9 us: dense_send(): pl.pallas_call(dense_send_kernel, grid=(groups,), in_specs=[row_block, an...]
    all_to_all x8 -> x1, waiting for transfers between devices: 53 us -> 17.7 us  [exchange(): return lax.all_to_all(blocks, 'seq', 0, 0, tiled=True)]
    all_to_all x8 -> x1, starting transfers between devices: 36.2 us -> 4.67 us  [exchange(): return lax.all_to_all(blocks, 'seq', 0, 0, tiled=True)]
    pallas_call x3 -> x1, Pallas kernels: 46.4 us -> 34.4 us  [attend(): pl.pallas_call(attend_kernel, grid_spec=pltpu.PrefetchScalarGridSpec(num_...]
    unnamed x52 -> x33, local copies, waits for them, and re-layouts: 20 us -> 11.7 us
    pallas_call x3 -> x1, Pallas kernels: 45 us -> 37.4 us  [attend_back(): pl.pallas_call(attend_back_kernel, grid_spec=pltpu.PrefetchScalarGridSpec...]
    all_to_all x4 -> x2, blocking collectives: 75 us -> 70 us  [exchange(): return lax.all_to_all(blocks, 'seq', 0, 0, tiled=True)]
  transfers between devices with their start and end apart: 9 -> 2, of which waited for: 5 -> 1; matrix products, arithmetic and copies ran while one was open for 3% -> 3% of each run, Pallas kernels for 24% -> 13%
where the time goes in v1:
time: 436 us; the launch traced here: 434 us
  Pallas kernels  290 us (67%)
  blocking collectives  70 us (16%)
  local copies, waits for them, and re-layouts  28.8 us (7%)
  waiting for transfers between devices  17.7 us (4%)
  between operations  14.9 us (3%)
  other arithmetic  7.81 us (2%)
  starting transfers between devices  4.7 us (1%)
    all_to_all x2, blocking collectives, exchange(): return lax.all_to_all(blocks, 'seq', 0, 0, tiled=True)  70 us
    pallas_call x1, Pallas kernels, dense_send(): pl.pallas_call(dense_send_kernel, grid=(groups,), in_specs=[row_block, an...  57.9 us
    pallas_call x1, Pallas kernels, project_send(): pl.pallas_call(project_send_kernel, grid=(groups,), in_specs=[pl.BlockSpe...  57 us
    pallas_call x1, Pallas kernels, sum_over_devices(): pl.pallas_call(sum_kernel, in_specs=[vmem, vmem, vmem], out_specs=[vmem,...  56.9 us
    pallas_call x1, Pallas kernels, attend_back(): pl.pallas_call(attend_back_kernel, grid_spec=pltpu.PrefetchScalarGridSpec...  37.4 us
    pallas_call x1, Pallas kernels, attend(): pl.pallas_call(attend_kernel, grid_spec=pltpu.PrefetchScalarGridSpec(num_...  34.4 us
    pallas_call x1, Pallas kernels, feed_grads(): pl.pallas_call(feed_grads_kernel, grid=(2, 4), in_specs=[pl.BlockSpec((gr...  21.9 us
    pallas_call x1, Pallas kernels, input_grads(): pl.pallas_call(input_grads_kernel, grid=(PAIRS,), in_specs=[pl.BlockSpec(...  19.7 us
  transfers between devices with their start and end apart: 2, of which 1 were waited for; matrix products, arithmetic and copies ran while one was open for 3% of the time, Pallas kernels for 13%

profile of v1, /device:TPU:0, one launch (start us, length us, event | category | flops | bytes accessed | tf_op | source)
XLA Modules:
  0.0 433.9 jit_solution(9950574996166742038)
XLA Ops:
  7.2 0.0 reduce-scatter.2.cloned.1.call-start
  7.2 0.1 add_select_fusion
  7.4 1.3 gather_fusion
  8.7 0.1 copy.23
  8.8 0.7 reshape.181.gain_ref
  9.5 0.0 copy-start.9
  9.5 0.7 reshape.197
  10.3 0.8 select_bitcast_fusion
  11.0 1.0 copy.25.weight_ref
  12.1 1.3 reshape.187.gain_ref
  13.3 0.1 pad_add_fusion.info
  13.4 0.0 copy-start.1
  13.4 2.0 copy-done.1
  15.4 0.0 copy-start.2
  15.4 1.4 copy-done.2
  16.8 57.0 %project_send.1 = (bf16[4,256,768]{2,1,0:T(8,128)(2,1)S(1)}, bf16[3,8,256,384]{3,2,1,0:T(8,128)(2,1)S(1)}) custom-call(bf16[4,256,768]{2,1,0:T(8,128)(2,1)S(1)} %copy-done.2, bf16[1,768]{1,0:T(2,128)(2,1)S(1)} %reshape.181.gain_ref, bf16[768,2304]{1,0:T(8,128)(2,1)S(1)} %copy-done.1), custom_call_target="tpu_custom_call" | custom-call | tf_op jit(solution)/shard_map/project_send/pallas_call | solution.py:176
  73.8 0.0 copy-done.9
  73.8 0.0 copy-start.6
  73.8 1.1 copy-done.6
  75.0 0.0 copy-start
  75.0 34.4 %attend.1 = (bf16[3,2048,128]{2,1,0:T(8,128)(2,1)S(1)}, f32[3,8,512]{2,1,0:T(8,128)S(1)}) custom-call(s32[3,2]{1,0:T(4,128)S(1)} %pad_add_fusion.info, bf16[3,2048,384]{2,1,0:T(8,128)(2,1)S(1)} %bitcast.42, f32[6,3,384]{2,1,0:T(4,128)S(1)} %reshape.194.taps_ref), custom_call_target="tpu_custom_call" | custom-call | tf_op jit(solution)/shard_map/attend/pallas_call | solution.py:318
  109.4 0.0 copy-done
  109.4 0.0 copy-start.3
  109.4 1.1 copy-done.3
  110.5 57.9 %dense_send.1 = (bf16[4,256,768]{2,1,0:T(8,128)(2,1)}, f32[4,256,768]{2,1,0:T(8,128)}, bf16[3,8,256,128]{3,2,1,0:T(8,128)(2,1)}, bf16[24,256,128]{2,1,0:T(8,128)...) custom-call(bf16[4,256,768]{2,1,0:T(8,128)(2,1)} %x_ref.5, ...), custom_call_target="tpu_custom_call" | custom-call | tf_op jit(solution)/shard_map/dense_send/pallas_call | solution.py:562
  168.4 21.9 %feed_grads.1 = bf16[8,4,432,384]{3,2,1,0:T(8,128)(2,1)} custom-call(bf16[4,256,3072]{2,1,0:T(8,128)(2,1)} %get-tuple-element.47.sq_ref, bf16[4,256,768]{2,1,0:T(8,128)(2,1)} %get-tuple-element.48.cz_ref, bf16[4,256,768]{2,1,0:T(8,128)(2,1)} %get-tuple-element.49.n2_ref, bf16[4,256,3072]{2,1,0:T(8,128)(2,1)} %get-tuple-element.50.du_ref, ...), custom_call_target="tpu_custom_call" | custom-call | tf_op jit(solution)/shard_map/feed_grads/pallas_call | solution.py:707
  190.4 0.0 copy-start.4
  190.4 0.0 copy-start.7
  190.4 0.0 reduce-scatter.2.cloned.1.call-update
  190.4 1.4 copy-done.4
  191.8 0.5 copy-done.7
  192.3 37.4 %attend_back.1 = (bf16[3,2048,384]{2,1,0:T(8,128)(2,1)}, f32[3,8,384]{2,1,0:T(8,128)S(1)}) custom-call(s32[3,2]{1,0:T(4,128)S(1)} %pad_add_fusion.info, bf16[3,2048,384]{2,1,0:T(8,128)(2,1)} %bitcast.43, f32[6,3,384]{2,1,0:T(4,128)S(1)} %reshape.194.taps_ref, bf16[3,2048,128]{2,1,0:T(8,128)(2,1)S(1)} %copy-done.4, bf16[3,2048,128]{2,1,0:T(8,128)(2,1)S(1)} %bitcast.45, ...), custom_call_target="tpu_custom_call" | custom-call | tf_op jit(solution)/shard_map/attend_back/pallas_call | solution.py:423
  229.6 4.3 fusion.8
  233.9 34.3 %all_to_all.15 = bf16[8,256,384]{2,1,0:T(8,128)(2,1)S(1)} all-to-all(bf16[8,256,384]{2,1,0:T(8,128)(2,1)S(1)} %bitcast.49), channel_id=1, replica_groups=mesh['seq'=8,'batch'=4] {'seq'}, dimensions={0} | all-to-all | bytes 3145728 | tf_op jit(solution)/shard_map/all_to_all | solution.py:1040
  268.2 35.7 %all_to_all.16 = bf16[8,256,384]{2,1,0:T(8,128)(2,1)S(1)} all-to-all(bf16[8,256,384]{2,1,0:T(8,128)(2,1)S(1)} %bitcast.48), channel_id=1, replica_groups=mesh['seq'=8,'batch'=4] {'seq'}, dimensions={0} | all-to-all | bytes 3145728 | tf_op jit(solution)/shard_map/all_to_all | solution.py:1040
  303.9 0.0 copy-start.12
  303.9 4.7 %all-to-all-start.2 = ((bf16[8,256,384]{2,1,0:T(8,128)(2,1)}), bf16[8,256,384]{2,1,0:T(8,128)(2,1)}, u32[]{:S(2)}, u32[]{:S(2)}) async-start(bf16[8,256,384]{2,1,0:T(8,128)(2,1)} %bitcast.47), calls=%async_computation.2 | async-start | bytes 3145728 | tf_op jit(solution)/shard_map/all_to_all | solution.py:1040
  308.8 0.0 copy-done.12
  308.8 0.1 slice_reduce_fusion
  309.0 0.6 fusion.11
  309.6 0.6 iota_compare_fusion
  310.2 0.7 iota_compare_fusion.1
  310.9 0.7 iota_compare_fusion.2
  311.5 0.1 broadcast_bitcast_fusion.2
  311.6 0.1 broadcast_bitcast_fusion
  311.7 17.7 %all-to-all-done.2 = bf16[8,256,384]{2,1,0:T(8,128)(2,1)} async-done(((bf16[8,256,384]{2,1,0:T(8,128)(2,1)}), bf16[8,256,384]{2,1,0:T(8,128)(2,1)}, u32[]{:S(2)}, u32[]{:S(2)}) %all-to-all-start.2) | async-done | bytes 1572896 | tf_op jit(solution)/shard_map/all_to_all | solution.py:1040
  329.4 3.6 pad_maximum_fusion
  333.1 0.0 copy-start.11
  333.1 19.7 %input_grads.1 = (bf16[3,2,4,4,48,384]{5,4,3,2,1,0:T(8,128)(2,1)}, f32[4,256,768]{2,1,0:T(8,128)}, f32[1,768]{1,0:T(1,128)}) custom-call(bf16[4,6,256,384]{3,2,1,0:T(8,128)(2,1)} %bitcast.46, bf16[4,256,768]{2,1,0:T(8,128)(2,1)} %copy-done.6, bf16[4,256,768]{2,1,0:T(8,128)(2,1)} %x_ref.5, f32[4,256,768]{2,1,0:T(8,128)} %get-tuple-element.44.dh_ref, ...), custom_call_target="tpu_custom_call" | custom-call | tf_op jit(solution)/shard_map/input_grads/pallas_call | solution.py:774
  352.8 0.0 copy-done.11
  352.8 2.0 concatenate.7.small_ref
  354.8 0.0 reduce-scatter.2.cloned.1.call-done
  354.8 56.9 %sum_over_devices.1 = (bf16[3,8,48,384]{3,2,1,0:T(8,128)(2,1)}, bf16[3,8,144,384]{3,2,1,0:T(8,128)(2,1)}, f32[16,768]{1,0:T(8,128)}) custom-call(bf16[3,2,4,4,48,384]{5,4,3,2,1,0:T(8,128)(2,1)} %get-tuple-element.46.g_ref, bf16[4,432,384]{2,1,0:T(8,128)(2,1)} %bitcast.51, f32[16,768]{1,0:T(8,128)} %concatenate.7.small_ref), custom_call_target="tpu_custom_call" | custom-call | tf_op jit(solution)/shard_map/sum_over_devices/pallas_call | solution.py:962
  411.7 1.3 slice.65
  413.0 0.8 fusion.9
  414.4 1.2 sqrt_bitcast_fusion
  415.6 1.4 reshape.192
  417.1 0.6 constant_dynamic-slice_fusion
  417.7 0.6 constant_dynamic-slice_fusion.1
  418.4 1.7 copy-done.5
  420.1 1.2 copy-done.8
  421.3 4.6 %unpack.1 = (f32[768,768]{1,0:T(8,128)}, f32[192,3072]{1,0:T(8,128)}, f32[192,768]{1,0:T(8,128)}, f32[192,2304]{1,0:T(8,128)}) custom-call(bf16[3,8,144,384]{3,2,1,0:T(8,128)(2,1)S(1)} %copy-done.5, bf16[3,8,48,384]{3,2,1,0:T(8,128)(2,1)S(1)} %copy-done.8), custom_call_target="tpu_custom_call" | custom-call | tf_op jit(solution)/shard_map/unpack/pallas_call | solution.py:1015
  425.9 0.0 copy-done.10
  425.9 1.1 copy.32
  (26 shorter events, 0.2 us)
Async XLA Ops:
  7.2 347.6 %reduce-scatter.2.cloned.1.call-start = ((), (), s32[]{:S(2)}) async-start(), calls=%async_computation.4 | async-start | bytes 11943936 | tf_op jit(solution)/shard_map/reduce_scatter | solution.py:1119
  9.5 64.4 %copy-start.9 = (bf16[1,768]{1,0:T(2,128)(2,1)}, bf16[1,768]{1,0:T(2,128)(2,1)S(1)}, u32[]{:S(2)}) copy-start(bf16[1,768]{1,0:T(2,128)(2,1)S(1)} %reshape.181.gain_ref) | copy-start | bytes 4612
  13.4 2.0 copy-start.1
  15.4 1.4 copy-start.2
  73.8 1.1 copy-start.6
  75.0 34.4 %copy-start = (bf16[3,8,256,384]{3,2,1,0:T(8,128)(2,1)}, bf16[3,8,256,384]{3,2,1,0:T(8,128)(2,1)S(1)}, u32[]{:S(2)}) copy-start(bf16[3,8,256,384]{3,2,1,0:T(8,128)(2,1)S(1)} %get-tuple-element.37) | copy-start | bytes 14155780
  109.4 1.1 copy-start.3
  190.4 1.4 copy-start.4
  190.4 1.9 copy-start.7
  303.9 4.9 %copy-start.12 = (f32[8,128]{1,0:T(8,128)S(1)}, f32[8,128]{1,0:T(8,128)}, u32[]{:S(2)}) copy-start(f32[8,128]{1,0:T(8,128)} %get-tuple-element.56) | copy-start | bytes 12292
  303.9 25.5 %all-to-all-start.2 = ((bf16[8,256,384]{2,1,0:T(8,128)(2,1)}), bf16[8,256,384]{2,1,0:T(8,128)(2,1)}, u32[]{:S(2)}, u32[]{:S(2)}) async-start(bf16[8,256,384]{2,1,0:T(8,128)(2,1)} %bitcast.47), calls=%async_computation.2 | async-start | bytes 3145728 | tf_op jit(solution)/shard_map/all_to_all | solution.py:1040
  333.1 19.7 %copy-start.11 = (f32[1,768]{1,0:T(1,128)S(1)}, f32[1,768]{1,0:T(1,128)}, u32[]{:S(2)}) copy-start(f32[1,768]{1,0:T(1,128)} %get-tuple-element.55) | copy-start | bytes 9220
  418.4 1.7 copy-start.5
  420.1 1.2 copy-start.8
  421.3 4.6 %copy-start.10 = (bf16[4,256,768]{2,1,0:T(8,128)(2,1)S(1)}, bf16[4,256,768]{2,1,0:T(8,128)(2,1)}, u32[]{:S(2)}) copy-start(bf16[4,256,768]{2,1,0:T(8,128)(2,1)} %get-tuple-element.89) | copy-start | bytes 4718596
Sparse Core Ops, SparseCore 0:
  190.5 116.1 reduce-scatter.1
